TPU v7x, 256 devices: a whole 4x4x8 slice. The times are simulated.
256 devices in a mesh: srv: 2 (over core), smp: 128 (over y, z, x).
Axes of the slice: x: 4, y: 4, z: 8, core: 2. Of those that a mesh axis runs over, the one named last changes fastest.
Arguments:
- genotype_sites: float32 [2, 1024, 32768], P('srv', None, 'smp'), may hold values from -6 to 8, as said below
- covariate_sites: float32 [2, 10, 32768], P('srv', None, 'smp'), may hold values from -8 to 10
- sample_ids: int32 [32768], P('smp'), may hold values from -1 to 16383, as said below
- mask_cov_first: float32 [2, 10, 16384], P('srv', None, 'smp'), may hold values from -6 to 6
- mask_geno: float32 [2, 1024, 16384], P('srv', None, 'smp'), may hold values from -6 to 6
- prod_first: float32 [2, 10, 1024], P('srv'), as said below
- mask_cov_second: float32 [2, 10, 16384], P('srv', None, 'smp'), may hold values from -6 to 6
- mask_weight: float32 [2, 10, 1024], P('srv'), may hold values from -6 to 6
- prod_second: float32 [2, 1024, 16384], P('srv', None, 'smp'), as said below
- coef: float32 [10, 10], replicated
- phenotypes: float32 [16384, 32], P('smp'), may hold values from -6 to 6
Outputs:
- residual_share: float32 [2, 1024, 16384], P('srv', 'smp')
- score_share: float32 [2, 1024, 32], P('srv', 'smp')
Inputs may be any that keep to these rules, and one draw needn't show every extreme that they name: `sample_ids`: every individual 0 to 16383 is named exactly once, all other entries are -1. Individual i belongs to sample block i // 128. Of the 256 entries of one device at most 2 belong to one sample block, and every block has a device with exactly 2 of them. `genotype_sites`: the two servers' shares add up to genotypes 0, 1 or 2. `prod_first`: the two shares add up to the product of the summed covariate mask and the summed genotype mask over all individuals. `prod_second`: the two shares add up to the summed coefficient mask transposed times the summed covariate mask.
All inputs are finite; a program needn't handle non-finite values.
Results may differ from a plain program's by a relative error of at most 0.0001.
Values sent between devices are 32-bit elements; how exact they have to be, the bound alone decides.
No kernel may reach another device: no remote copies, remote signals or barrier semaphores. Data moves between devices by JAX's collectives and lax.ppermute only.
A program may use at most 64 MiB of HBM per device.

v0:
```python
import math

import jax
import jax.numpy as jnp
from jax import lax
from jax.experimental import pallas as pl
from jax.experimental.pallas import tpu as pltpu
from jax.sharding import PartitionSpec as P


K = 10
LANES = 128
PHEN = 32
HIGH = lax.Precision.HIGHEST
NT = (((1,), (1,)), ((), ()))
TN = (((0,), (0,)), ((), ()))
VMEM = pl.BlockSpec(memory_space=pltpu.VMEM)
TIGHT = pltpu.CompilerParams(vmem_limit_bytes=67043328)
ROOM = pltpu.CompilerParams(vmem_limit_bytes=16 << 20)


def parts(x):
    high = x.astype(jnp.bfloat16)
    rest = x - high.astype(jnp.float32)
    mid = rest.astype(jnp.bfloat16)
    low = (rest - mid.astype(jnp.float32)).astype(jnp.bfloat16)
    return high, mid, low


def mm(left, right, dims):
    return lax.dot_general(left, right, dims, preferred_element_type=jnp.float32)


def pad_rows(x, rows):
    return jnp.concatenate([x, jnp.zeros((rows - x.shape[0], x.shape[1]), x.dtype)], axis=0)


def chunk_of(ref, c):
    return ref[pl.ds(c, K, stride=ref.shape[0] // K), :]


def plain(ref):
    return jnp.concatenate([ref[k] for k in range(ref.shape[0])], axis=0)


def pack_kernel(
    ids, geno, cov, cov_peer, mcf, mcf_peer, mg, prod_first, mw, coef, payload, weight
):
    width = geno.shape[2]
    chunks = geno.shape[1] // LANES
    rows = 2 * chunks + 1
    first = (lax.axis_index("smp") == 0).astype(jnp.float32)
    ident = ids[...]
    live = ident >= 0
    block = jnp.where(live, lax.shift_right_arithmetic(ident, 7), -1)
    spot = jnp.where(live, lax.bitwise_and(ident, 127) + 1, 0)
    block_rows = jnp.broadcast_to(block.astype(jnp.float32), (width, width))
    same = block_rows == block_rows.T
    earlier = lax.broadcasted_iota(jnp.int32, (width, width), 0) < lax.broadcasted_iota(
        jnp.int32, (width, width), 1
    )
    rank = jnp.sum(jnp.where(same & earlier, 1.0, 0.0), axis=0, keepdims=True)
    hit = lax.broadcasted_iota(jnp.int32, (LANES, width), 0) == jnp.broadcast_to(
        block, (LANES, width)
    )
    rank_rows = jnp.broadcast_to(rank, (LANES, width))
    one = jnp.float32(1.0)
    pick = [
        jnp.where(hit & (rank_rows == float(slot)), one, 0.0).astype(jnp.bfloat16)
        for slot in range(2)
    ]
    cov_sum = jnp.where(live, plain(cov) + plain(cov_peer), 0.0)
    cov_parts = parts(pad_rows(cov_sum, 16))
    left = jnp.concatenate([*pick, *cov_parts], axis=0)
    mcf_left = jnp.concatenate(parts(pad_rows(plain(mcf) + plain(mcf_peer), 16)), axis=0)
    table = coef[...]
    base = 2 * LANES
    for c in range(chunks):
        cols = pl.ds(c * LANES, LANES)
        got = sum(mm(left, piece, NT) for piece in parts(geno[0, cols, :]))
        payload[pl.ds(c, LANES, stride=rows), :] = got[:LANES]
        payload[pl.ds(chunks + c, LANES, stride=rows), :] = got[LANES:base]
        gram = got[base:] - sum(mm(mcf_left, piece, NT) for piece in parts(mg[0, cols, :]))
        gram = gram[:16] + gram[16:32] + gram[32:48]
        gram = gram[:K] + first * chunk_of(prod_first, c)
        out = -first * chunk_of(mw, c)
        for k in range(K):
            out = out + table[:, k : k + 1] * gram[k : k + 1, :]
        weight[pl.ds(c * K, K), :] = out
    side = jnp.concatenate(
        [cov_sum, spot.astype(jnp.float32), jnp.zeros((64 - K - 1, width), jnp.float32)], axis=0
    )
    blank = jnp.zeros_like(side)
    extra = jnp.zeros((LANES, LANES), jnp.float32)
    for slot in range(2):
        both = jnp.concatenate([side, blank] if slot == 0 else [blank, side], axis=0)
        for piece in parts(both):
            extra = extra + mm(pick[slot], piece, NT)
    payload[pl.ds(2 * chunks, LANES, stride=rows), :] = extra


def fit_kernel(recv, w_0, w_1, w_2, w_3, mw, mcs, mcs_peer, prod_second, phen, payload, a_s, b_s):
    variants = prod_second.shape[1]
    chunks = variants // LANES
    rows = 2 * chunks + 1
    out_rows = 8 + 2
    leader = (lax.axis_index("srv") == 0).astype(jnp.float32)
    sources = recv.shape[0] // rows
    extra = recv[pl.ds(2 * chunks, sources, stride=rows), :]
    lane = lax.broadcasted_iota(jnp.int32, (sources, LANES), 1)
    place = []
    for slot in range(2):
        at = extra[:, 64 * slot + K : 64 * slot + K + 1].astype(jnp.int32) - 1
        place.append(jnp.where(lane == at, jnp.float32(1.0), 0.0).astype(jnp.bfloat16))
    cov = jnp.zeros((16, LANES), jnp.float32)
    for slot in range(2):
        for piece in parts(extra):
            cov = cov + mm(piece, place[slot], TN)[64 * slot : 64 * slot + 16]
    own_mask = plain(mcs)
    open_second = cov[:K] - own_mask - plain(mcs_peer)
    b_s[...] = jnp.zeros_like(b_s)
    b_s[0:K, :] = open_second
    b_s[16 : 16 + K, :] = own_mask + leader * open_second
    a_s[...] = jnp.zeros_like(a_s)
    ow = w_0[...] + w_1[...] + w_2[...] + w_3[...]
    for c in range(chunks):
        a_s[0:K, pl.ds(c * LANES, LANES)] = chunk_of(mw, c)
        a_s[16 : 16 + K, pl.ds(c * LANES, LANES)] = ow[c * K : (c + 1) * K]
    spots = jnp.concatenate(place, axis=0)
    b_all = b_s[...]
    for c in range(chunks):
        cols = pl.ds(c * LANES, LANES)
        sent = jnp.concatenate(
            [
                recv[pl.ds(c, sources, stride=rows), :],
                recv[pl.ds(chunks + c, sources, stride=rows), :],
            ],
            axis=0,
        )
        geno = sum(mm(piece, spots, TN) for piece in parts(sent))
        fitted = prod_second[0, cols, :] + lax.dot_general(
            a_s[:, cols], b_all, TN, precision=HIGH, preferred_element_type=jnp.float32
        )
        residual = geno - fitted
        for t in range(LANES // 8):
            payload[pl.ds((c * (LANES // 8) + t) * out_rows, 8), :] = residual[8 * t : 8 * t + 8]
    owners = payload.shape[0] // out_rows
    group = LANES // PHEN
    wide = phen[...]
    blank = jnp.zeros_like(wide)
    shifted = [
        jnp.concatenate([wide if g == at else blank for at in range(group)], axis=0)
        for g in range(group)
    ]
    for half in range(8 // group):
        total = jnp.zeros((owners, LANES), jnp.float32)
        for g in range(group):
            total = total + lax.dot_general(
                payload[pl.ds(half * group + g, owners, stride=out_rows), :],
                shifted[g],
                NT,
                precision=HIGH,
                preferred_element_type=jnp.float32,
            )
        payload[pl.ds(8 + half, owners, stride=out_rows), :] = total


def finish_kernel(scale, recv, columns, score):
    out_rows = 10
    sources = recv.shape[0] // out_rows
    for s in range(sources):
        columns[0, :, pl.ds(s * LANES, LANES)] = recv[pl.ds(s * out_rows, 8), :]
    group = LANES // PHEN
    for half in range(8 // group):
        total = jnp.sum(recv[pl.ds(8 + half, sources, stride=out_rows), :], axis=0, keepdims=True)
        total = total * scale
        for g in range(group):
            score[0, pl.ds(half * group + g, 1), :] = total[:, g * PHEN : (g + 1) * PHEN]


def swap(value):
    return lax.ppermute(value, "srv", [(0, 1), (1, 0)])


def index(y, z, x):
    return ((y % 4) * 8 + z % 8) * 4 + x % 4


def shifted(value, dy, dz, dx):
    pairs = [
        (index(y, z, x), index(y + dy, z + dz, x + dx))
        for y in range(4)
        for z in range(8)
        for x in range(4)
    ]
    return lax.ppermute(value, "smp", pairs)


def z_pair(value):
    return lax.ppermute(value, "smp", [(i, i ^ 4) for i in range(lax.axis_size("smp"))])


def terms(value, *moves):
    return [value] + [shifted(value, *move) for move in moves]


def total(values):
    return values[0] + values[1] + values[2] + values[3]


def rows_of(value):
    return value.reshape(-1, LANES)


def exchange(rows, peers):
    per = rows.shape[0] // peers
    flat = rows.reshape(peers, 1, per * LANES)
    got = lax.all_to_all(flat, "smp", split_axis=0, concat_axis=0, tiled=True)
    return got.reshape(peers * per, LANES)


def local(
    genotype_sites,
    covariate_sites,
    sample_ids,
    mask_cov_first,
    mask_geno,
    prod_first,
    mask_cov_second,
    mask_weight,
    prod_second,
    coef,
    phenotypes,
):
    peers = lax.axis_size("smp")
    variants = genotype_sites.shape[1]
    chunks = variants // LANES
    cov, mcf, mcs = (
        value.transpose(1, 0, 2) for value in (covariate_sites, mask_cov_first, mask_cov_second)
    )
    cov_peer, mcf_peer = swap((cov, mcf))
    first_product, mw = (rows_of(value.transpose(1, 0, 2)) for value in (prod_first, mask_weight))
    packed, weight = pl.pallas_call(
        pack_kernel,
        out_shape=(
            jax.ShapeDtypeStruct((peers * (2 * chunks + 1), LANES), jnp.float32),
            jax.ShapeDtypeStruct((chunks * K, LANES), jnp.float32),
        ),
        in_specs=[VMEM] * 10,
        out_specs=(VMEM, VMEM),
        compiler_params=TIGHT,
    )(
        sample_ids[None],
        genotype_sites,
        cov,
        cov_peer,
        mcf,
        mcf_peer,
        mask_geno,
        first_product,
        mw,
        coef,
    )
    received = exchange(packed, peers)
    other = z_pair(weight)
    weight = weight + other
    weight = weight + swap(weight)
    mcs_peer = swap(mcs)
    weight, mcs_peer = lax.optimization_barrier((weight, mcs_peer))
    weight = total(terms(weight, (0, 0, 1), (0, 0, 3), (0, 0, 2)))
    weight = total(terms(weight, (1, 0, 0), (3, 0, 0), (2, 0, 0)))
    open_weight = terms(weight, (0, 2, 0), (0, 6, 0), (0, 4, 0))
    fitted = pl.pallas_call(
        fit_kernel,
        out_shape=jax.ShapeDtypeStruct((variants // 8 * 10, LANES), jnp.float32),
        in_specs=[VMEM] * 10,
        out_specs=VMEM,
        compiler_params=ROOM,
        scratch_shapes=[
            pltpu.VMEM((32, variants), jnp.float32),
            pltpu.VMEM((32, LANES), jnp.float32),
        ],
    )(received, *open_weight, mw, mcs, mcs_peer, prod_second, phenotypes.T)
    gathered = exchange(fitted, peers)
    scale = 1.0 / math.sqrt(peers * LANES)
    return pl.pallas_call(
        lambda *refs: finish_kernel(scale, *refs),
        out_shape=(
            jax.ShapeDtypeStruct((1, 8, peers * LANES), jnp.float32),
            jax.ShapeDtypeStruct((1, 8, PHEN), jnp.float32),
        ),
        in_specs=[VMEM],
        out_specs=(VMEM, VMEM),
        compiler_params=ROOM,
    )(gathered)


def solution(mesh):
    return jax.shard_map(
        local,
        mesh=mesh,
        in_specs=(
            P("srv", None, "smp"),
            P("srv", None, "smp"),
            P("smp"),
            P("srv", None, "smp"),
            P("srv", None, "smp"),
            P("srv", None, None),
            P("srv", None, "smp"),
            P("srv", None, None),
            P("srv", None, "smp"),
            P(),
            P("smp", None),
        ),
        out_specs=(P("srv", "smp", None), P("srv", "smp", None)),
        check_vma=False,
    )
```

profile of v0, /device:TPU:32, one launch (start us, length us, event | category | flops | bytes accessed | tf_op | source)
XLA Modules:
  0.0 109.1 jit_solution(586985048218327793)
XLA Ops:
  0.6 0.1 collective-permute-start
  0.7 0.5 collective-permute-start.1
  1.2 1.2 %collective-permute-done.1.mcf_peer = f32[10,1,128]{2,1,0:T(1,128)} collective-permute-done((f32[10,1,128]{2,1,0:T(1,128)}, f32[10,1,128]{2,1,0:T(1,128)}, u32[]{:S(2)}, u32[]{:S(2)}) %collective-permute-start.1) | collective-permute-done | bytes 5152 | tf_op jit(solution)/shard_map/ppermute | solution.py:182
  2.4 4.3 %shard_map.122 = (f32[2176,128]{1,0:T(8,128)}, f32[80,128]{1,0:T(8,128)}) custom-call(s32[1,256]{1,0:T(1,128)} %bitcast.25, f32[1,1024,256]{2,1,0:T(8,128)} %geno.1, f32[10,1,256]{2,1,0:T(1,128)} %bitcast.22, f32[10,1,256]{2,1,0:T(1,128)} %collective-permute-done.cov_peer, f32[10,1,128]{2,1,0:T(1,128)} %bitcast.24, ...), custom_call_target="tpu_custom_call" | custom-call | tf_op jit(solution)/shard_map/pallas_call | solution.py:243
  6.7 0.0 copy-start
  6.7 0.0 copy-start.1
  6.7 0.0 copy-start.2
  6.7 15.1 %all-to-all-start = ((f32[128,1,2176]{2,1,0:T(1,128)}), f32[128,1,2176]{2,1,0:T(1,128)S(1)}, u32[]{:S(2)}, u32[]{:S(2)}) async-start(f32[128,1,2176]{2,1,0:T(1,128)} %bitcast.19), calls=%async_computation | async-start | bytes 2228224 | tf_op jit(solution)/shard_map/all_to_all | solution.py:218
  21.9 1.0 collective-permute-start.2
  22.9 24.4 %collective-permute-done.2 = f32[80,128]{1,0:T(8,128)S(1)} collective-permute-done((f32[80,128]{1,0:T(8,128)S(1)}, f32[80,128]{1,0:T(8,128)S(1)}, u32[]{:S(2)}, u32[]{:S(2)}) %collective-permute-start.2) | collective-permute-done | bytes 40992 | tf_op jit(solution)/shard_map/ppermute | solution.py:200
  47.3 0.5 collective-permute-start.4
  47.8 0.7 collective-permute-done.3
  48.5 0.1 collective-permute-done.4.mcs_peer
  48.6 2.1 %collective-permute-start.7 = (f32[80,128]{1,0:T(8,128)S(1)}, f32[80,128]{1,0:T(8,128)S(1)}, u32[]{:S(2)}, u32[]{:S(2)}) collective-permute-start(f32[80,128]{1,0:T(8,128)S(1)} %add.25), channel_id=1, source_target_pairs={{0,2},{1,3},{2,0},{3,1},{4,6},{5,7},{6,4},{7,5},{8,10},{9,11},{10,... | collective-permute-start | bytes 122888 | tf_op jit(solution)/shard_map/ppermute | solution.py:196
  50.7 1.5 %collective-permute-start.6 = (f32[80,128]{1,0:T(8,128)S(1)}, f32[80,128]{1,0:T(8,128)S(1)}, u32[]{:S(2)}, u32[]{:S(2)}) collective-permute-start(f32[80,128]{1,0:T(8,128)S(1)} %add.25), channel_id=1, source_target_pairs={{0,3},{1,0},{2,1},{3,2},{4,7},{5,4},{6,5},{7,6},{8,11},{9,8},{10,9... | collective-permute-start | bytes 122888 | tf_op jit(solution)/shard_map/ppermute | solution.py:196
  52.2 0.6 collective-permute-start.5
  52.7 1.4 %collective-permute-done.7 = f32[80,128]{1,0:T(8,128)S(1)} collective-permute-done((f32[80,128]{1,0:T(8,128)S(1)}, f32[80,128]{1,0:T(8,128)S(1)}, u32[]{:S(2)}, u32[]{:S(2)}) %collective-permute-start.7) | collective-permute-done | bytes 40992 | tf_op jit(solution)/shard_map/ppermute | solution.py:196
  54.2 0.6 collective-permute-done.6
  54.7 2.7 %collective-permute-done.5 = f32[80,128]{1,0:T(8,128)S(1)} collective-permute-done((f32[80,128]{1,0:T(8,128)S(1)}, f32[80,128]{1,0:T(8,128)S(1)}, u32[]{:S(2)}, u32[]{:S(2)}) %collective-permute-start.5) | collective-permute-done | bytes 40992 | tf_op jit(solution)/shard_map/ppermute | solution.py:196
  57.4 3.3 %collective-permute-start.10 = (f32[80,128]{1,0:T(8,128)S(1)}, f32[80,128]{1,0:T(8,128)S(1)}, u32[]{:S(2)}, u32[]{:S(2)}) collective-permute-start(f32[80,128]{1,0:T(8,128)S(1)} %add_add_fusion.1), channel_id=1, source_target_pairs={{0,64},{1,65},{2,66},{3,67},{4,68},{5,69},{6,70},{7,71},{8,72},{9,... | collective-permute-start | bytes 122888 | tf_op jit(solution)/shard_map/ppermute | solution.py:196
  60.7 0.9 collective-permute-start.9
  61.7 1.1 collective-permute-start.8
  62.7 0.6 collective-permute-done.10
  63.4 1.4 %collective-permute-done.9 = f32[80,128]{1,0:T(8,128)S(1)} collective-permute-done((f32[80,128]{1,0:T(8,128)S(1)}, f32[80,128]{1,0:T(8,128)S(1)}, u32[]{:S(2)}, u32[]{:S(2)}) %collective-permute-start.9) | collective-permute-done | bytes 40992 | tf_op jit(solution)/shard_map/ppermute | solution.py:196
  64.7 2.2 %collective-permute-done.8 = f32[80,128]{1,0:T(8,128)S(1)} collective-permute-done((f32[80,128]{1,0:T(8,128)S(1)}, f32[80,128]{1,0:T(8,128)S(1)}, u32[]{:S(2)}, u32[]{:S(2)}) %collective-permute-start.8) | collective-permute-done | bytes 40992 | tf_op jit(solution)/shard_map/ppermute | solution.py:196
  66.9 3.0 %collective-permute-start.11 = (f32[80,128]{1,0:T(8,128)S(1)}, f32[80,128]{1,0:T(8,128)S(1)}, u32[]{:S(2)}, u32[]{:S(2)}) collective-permute-start(f32[80,128]{1,0:T(8,128)S(1)} %add_add_fusion.w_0), channel_id=1, source_target_pairs={{0,8},{1,9},{2,10},{3,11},{4,12},{5,13},{6,14},{7,15},{8,16},{9,17... | collective-permute-start | bytes 122888 | tf_op jit(solution)/shard_map/ppermute | solution.py:196
  69.8 1.3 %collective-permute-start.12 = (f32[80,128]{1,0:T(8,128)S(1)}, f32[80,128]{1,0:T(8,128)S(1)}, u32[]{:S(2)}, u32[]{:S(2)}) collective-permute-start(f32[80,128]{1,0:T(8,128)S(1)} %add_add_fusion.w_0), channel_id=1, source_target_pairs={{0,24},{1,25},{2,26},{3,27},{4,28},{5,29},{6,30},{7,31},{8,0},{9,1... | collective-permute-start | bytes 122888 | tf_op jit(solution)/shard_map/ppermute | solution.py:196
  71.1 6.0 %collective-permute-start.13 = (f32[80,128]{1,0:T(8,128)S(1)}, f32[80,128]{1,0:T(8,128)S(1)}, u32[]{:S(2)}, u32[]{:S(2)}) collective-permute-start(f32[80,128]{1,0:T(8,128)S(1)} %add_add_fusion.w_0), channel_id=1, source_target_pairs={{0,16},{1,17},{2,18},{3,19},{4,20},{5,21},{6,22},{7,23},{8,24},{9,... | collective-permute-start | bytes 122888 | tf_op jit(solution)/shard_map/ppermute | solution.py:196
  77.1 2.4 %collective-permute-done.13.w_3 = f32[80,128]{1,0:T(8,128)S(1)} collective-permute-done((f32[80,128]{1,0:T(8,128)S(1)}, f32[80,128]{1,0:T(8,128)S(1)}, u32[]{:S(2)}, u32[]{:S(2)}) %collective-permute-start.13) | collective-permute-done | bytes 40992 | tf_op jit(solution)/shard_map/ppermute | solution.py:196
  79.5 2.1 %shard_map.123 = f32[1280,128]{1,0:T(8,128)S(1)} custom-call(f32[2176,128]{1,0:T(8,128)S(1)} %bitcast.11, f32[80,128]{1,0:T(8,128)S(1)} %add_add_fusion.w_0, f32[80,128]{1,0:T(8,128)S(1)} %collective-permute-done.11.w_1, f32[80,128]{1,0:T(8,128)S(1)} %collective-permute-done.12.w_2, f32[80,128]{1,0:T(8,128)S(1)} %collective-permute-done.13.w_3, ...), custom_call_target="tpu_custom_call" | custom-call | tf_op jit(solution)/shard_map/pallas_call | solution.py:273
  81.6 26.6 %all_to_all.10 = f32[128,1,1280]{2,1,0:T(1,128)S(1)} all-to-all(f32[128,1,1280]{2,1,0:T(1,128)S(1)} %bitcast.13), channel_id=1, replica_groups=mesh['srv'=2,'smp'=128] {'smp'}, dimensions={0} | all-to-all | bytes 1310720 | tf_op jit(solution)/shard_map/all_to_all | solution.py:218
  108.2 0.8 shard_map.124
  (16 shorter events, 0.1 us)
Async XLA Ops:
  0.6 1.8 %collective-permute-start = (f32[10,1,256]{2,1,0:T(1,128)}, f32[10,1,256]{2,1,0:T(1,128)}, u32[]{:S(2)}, u32[]{:S(2)}) collective-permute-start(f32[10,1,256]{2,1,0:T(1,128)} %bitcast.21), channel_id=1, source_target_pairs={{0,128},{128,0},{1,129},{129,1},{2,130},{130,2},{3,131},{131,3},{4... | collective-permute-start | bytes 30728 | tf_op jit(solution)/shard_map/ppermute | solution.py:182
  0.7 1.7 %collective-permute-start.1 = (f32[10,1,128]{2,1,0:T(1,128)}, f32[10,1,128]{2,1,0:T(1,128)}, u32[]{:S(2)}, u32[]{:S(2)}) collective-permute-start(f32[10,1,128]{2,1,0:T(1,128)} %bitcast.23), channel_id=1, source_target_pairs={{0,128},{128,0},{1,129},{129,1},{2,130},{130,2},{3,131},{131,3},{4... | collective-permute-start | bytes 15368 | tf_op jit(solution)/shard_map/ppermute | solution.py:182
  6.7 15.2 %copy-start.4 = (f32[80,128]{1,0:T(8,128)S(1)}, f32[80,128]{1,0:T(8,128)}, u32[]{:S(2)}) copy-start(f32[80,128]{1,0:T(8,128)} %get-tuple-element.7) | copy-start | bytes 122884
  6.7 40.6 %copy-start.3 = (f32[1,10,128]{2,0,1:T(1,128)S(1)}, f32[1,10,128]{2,0,1:T(1,128)}, u32[]{:S(2)}) copy-start(f32[1,10,128]{2,0,1:T(1,128)} %param.17) | copy-start | bytes 15364
  6.7 72.8 %copy-start = (f32[1,1024,128]{2,1,0:T(8,128)S(1)}, f32[1,1024,128]{2,1,0:T(8,128)}, u32[]{:S(2)}) copy-start(f32[1,1024,128]{2,1,0:T(8,128)} %prod_second.1) | copy-start | bytes 1572868
  6.7 72.8 %copy-start.1 = (f32[1,10,1024]{2,0,1:T(1,128)S(1)}, f32[1,10,1024]{2,0,1:T(1,128)}, u32[]{:S(2)}) copy-start(f32[1,10,1024]{2,0,1:T(1,128)} %param.18) | copy-start | bytes 122884
  6.7 72.8 %copy-start.2 = (f32[128,32]{0,1:T(8,128)S(1)}, f32[128,32]{0,1:T(8,128)}, u32[]{:S(2)}) copy-start(f32[128,32]{0,1:T(8,128)} %param.21) | copy-start | bytes 49156
  6.7 72.8 %all-to-all-start = ((f32[128,1,2176]{2,1,0:T(1,128)}), f32[128,1,2176]{2,1,0:T(1,128)S(1)}, u32[]{:S(2)}, u32[]{:S(2)}) async-start(f32[128,1,2176]{2,1,0:T(1,128)} %bitcast.19), calls=%async_computation | async-start | bytes 2228224 | tf_op jit(solution)/shard_map/all_to_all | solution.py:218
  21.9 25.4 %collective-permute-start.2 = (f32[80,128]{1,0:T(8,128)S(1)}, f32[80,128]{1,0:T(8,128)S(1)}, u32[]{:S(2)}, u32[]{:S(2)}) collective-permute-start(f32[80,128]{1,0:T(8,128)S(1)} %copy-done.4), channel_id=1, source_target_pairs={{0,4},{1,5},{2,6},{3,7},{4,0},{5,1},{6,2},{7,3},{8,12},{9,13},{10,... | collective-permute-start | bytes 122888 | tf_op jit(solution)/shard_map/ppermute | solution.py:200
  47.3 1.2 %collective-permute-start.3 = (f32[80,128]{1,0:T(8,128)S(1)}, f32[80,128]{1,0:T(8,128)S(1)}, u32[]{:S(2)}, u32[]{:S(2)}) collective-permute-start(f32[80,128]{1,0:T(8,128)S(1)} %add.24), channel_id=1, source_target_pairs={{0,128},{128,0},{1,129},{129,1},{2,130},{130,2},{3,131},{131,3},{4... | collective-permute-start | bytes 122888 | tf_op jit(solution)/shard_map/ppermute | solution.py:182
  47.3 1.3 %collective-permute-start.4 = (f32[10,1,128]{2,1,0:T(1,128)S(1)}, f32[10,1,128]{2,1,0:T(1,128)S(1)}, u32[]{:S(2)}, u32[]{:S(2)}) collective-permute-start(f32[10,1,128]{2,1,0:T(1,128)S(1)} %bitcast.17), channel_id=1, source_target_pairs={{0,128},{128,0},{1,129},{129,1},{2,130},{130,2},{3,131},{131,3},{4... | collective-permute-start | bytes 15368 | tf_op jit(solution)/shard_map/ppermute | solution.py:182
  48.6 5.5 %collective-permute-start.7 = (f32[80,128]{1,0:T(8,128)S(1)}, f32[80,128]{1,0:T(8,128)S(1)}, u32[]{:S(2)}, u32[]{:S(2)}) collective-permute-start(f32[80,128]{1,0:T(8,128)S(1)} %add.25), channel_id=1, source_target_pairs={{0,2},{1,3},{2,0},{3,1},{4,6},{5,7},{6,4},{7,5},{8,10},{9,11},{10,... | collective-permute-start | bytes 122888 | tf_op jit(solution)/shard_map/ppermute | solution.py:196
  50.7 4.0 %collective-permute-start.6 = (f32[80,128]{1,0:T(8,128)S(1)}, f32[80,128]{1,0:T(8,128)S(1)}, u32[]{:S(2)}, u32[]{:S(2)}) collective-permute-start(f32[80,128]{1,0:T(8,128)S(1)} %add.25), channel_id=1, source_target_pairs={{0,3},{1,0},{2,1},{3,2},{4,7},{5,4},{6,5},{7,6},{8,11},{9,8},{10,9... | collective-permute-start | bytes 122888 | tf_op jit(solution)/shard_map/ppermute | solution.py:196
  52.2 5.2 %collective-permute-start.5 = (f32[80,128]{1,0:T(8,128)S(1)}, f32[80,128]{1,0:T(8,128)S(1)}, u32[]{:S(2)}, u32[]{:S(2)}) collective-permute-start(f32[80,128]{1,0:T(8,128)S(1)} %add.25), channel_id=1, source_target_pairs={{0,1},{1,2},{2,3},{3,0},{4,5},{5,6},{6,7},{7,4},{8,9},{9,10},{10,1... | collective-permute-start | bytes 122888 | tf_op jit(solution)/shard_map/ppermute | solution.py:196
  57.4 5.9 %collective-permute-start.10 = (f32[80,128]{1,0:T(8,128)S(1)}, f32[80,128]{1,0:T(8,128)S(1)}, u32[]{:S(2)}, u32[]{:S(2)}) collective-permute-start(f32[80,128]{1,0:T(8,128)S(1)} %add_add_fusion.1), channel_id=1, source_target_pairs={{0,64},{1,65},{2,66},{3,67},{4,68},{5,69},{6,70},{7,71},{8,72},{9,... | collective-permute-start | bytes 122888 | tf_op jit(solution)/shard_map/ppermute | solution.py:196
  60.7 4.0 %collective-permute-start.9 = (f32[80,128]{1,0:T(8,128)S(1)}, f32[80,128]{1,0:T(8,128)S(1)}, u32[]{:S(2)}, u32[]{:S(2)}) collective-permute-start(f32[80,128]{1,0:T(8,128)S(1)} %add_add_fusion.1), channel_id=1, source_target_pairs={{0,96},{1,97},{2,98},{3,99},{4,100},{5,101},{6,102},{7,103},{8,104... | collective-permute-start | bytes 122888 | tf_op jit(solution)/shard_map/ppermute | solution.py:196
  61.7 5.2 %collective-permute-start.8 = (f32[80,128]{1,0:T(8,128)S(1)}, f32[80,128]{1,0:T(8,128)S(1)}, u32[]{:S(2)}, u32[]{:S(2)}) collective-permute-start(f32[80,128]{1,0:T(8,128)S(1)} %add_add_fusion.1), channel_id=1, source_target_pairs={{0,32},{1,33},{2,34},{3,35},{4,36},{5,37},{6,38},{7,39},{8,40},{9,... | collective-permute-start | bytes 122888 | tf_op jit(solution)/shard_map/ppermute | solution.py:196
  66.9 10.2 %collective-permute-start.11 = (f32[80,128]{1,0:T(8,128)S(1)}, f32[80,128]{1,0:T(8,128)S(1)}, u32[]{:S(2)}, u32[]{:S(2)}) collective-permute-start(f32[80,128]{1,0:T(8,128)S(1)} %add_add_fusion.w_0), channel_id=1, source_target_pairs={{0,8},{1,9},{2,10},{3,11},{4,12},{5,13},{6,14},{7,15},{8,16},{9,17... | collective-permute-start | bytes 122888 | tf_op jit(solution)/shard_map/ppermute | solution.py:196
  69.8 7.2 %collective-permute-start.12 = (f32[80,128]{1,0:T(8,128)S(1)}, f32[80,128]{1,0:T(8,128)S(1)}, u32[]{:S(2)}, u32[]{:S(2)}) collective-permute-start(f32[80,128]{1,0:T(8,128)S(1)} %add_add_fusion.w_0), channel_id=1, source_target_pairs={{0,24},{1,25},{2,26},{3,27},{4,28},{5,29},{6,30},{7,31},{8,0},{9,1... | collective-permute-start | bytes 122888 | tf_op jit(solution)/shard_map/ppermute | solution.py:196
  71.1 8.4 %collective-permute-start.13 = (f32[80,128]{1,0:T(8,128)S(1)}, f32[80,128]{1,0:T(8,128)S(1)}, u32[]{:S(2)}, u32[]{:S(2)}) collective-permute-start(f32[80,128]{1,0:T(8,128)S(1)} %add_add_fusion.w_0), channel_id=1, source_target_pairs={{0,16},{1,17},{2,18},{3,19},{4,20},{5,21},{6,22},{7,23},{8,24},{9,... | collective-permute-start | bytes 122888 | tf_op jit(solution)/shard_map/ppermute | solution.py:196
where the time goes:
time: 109 us
  waiting for transfers between devices  37.6 us (34%)
  starting transfers between devices  36.8 us (34%)
  blocking collectives  26.6 us (24%)
  Pallas kernels  7.21 us (7%)
    all_to_all x1, blocking collectives, exchange(): got = lax.all_to_all(flat, 'smp', split_axis=0, concat_axis=0, tiled=True)  26.6 us
    ppermute x1, waiting for transfers between devices, z_pair(): lax.ppermute(value, 'smp', [(i, i ^ 4) for i in range(lax.axis_size('smp'...  24.4 us
    ppermute x9, starting transfers between devices, shifted(): return lax.ppermute(value, 'smp', pairs)  19.6 us
    all_to_all x1, starting transfers between devices, exchange(): got = lax.all_to_all(flat, 'smp', split_axis=0, concat_axis=0, tiled=True)  15.1 us
    ppermute x9, waiting for transfers between devices, shifted(): return lax.ppermute(value, 'smp', pairs)  11.2 us
    pallas_call x1, Pallas kernels, local(): pl.pallas_call(pack_kernel, out_shape=(jax.ShapeDtypeStruct((peers * (2 *...  4.27 us
  transfers between devices with their start and end apart: 15, of which 11 were waited for; matrix products, arithmetic and copies ran while one was open for 0% of the time, Pallas kernels for 0%

commit v1 on v0

--- a/solution.py
+++ b/solution.py
@@ -11,7 +11,6 @@
 K = 10
 LANES = 128
 PHEN = 32
-HIGH = lax.Precision.HIGHEST
 NT = (((1,), (1,)), ((), ()))
 TN = (((0,), (0,)), ((), ()))
 VMEM = pl.BlockSpec(memory_space=pltpu.VMEM)
@@ -25,6 +24,11 @@
     mid = rest.astype(jnp.bfloat16)
     low = (rest - mid.astype(jnp.float32)).astype(jnp.bfloat16)
     return high, mid, low
+
+
+def halves(x):
+    high = x.astype(jnp.bfloat16)
+    return high, (x - high.astype(jnp.float32)).astype(jnp.bfloat16)
 
 
 def mm(left, right, dims):
@@ -75,18 +79,22 @@
     mcf_left = jnp.concatenate(parts(pad_rows(plain(mcf) + plain(mcf_peer), 16)), axis=0)
     table = coef[...]
     base = 2 * LANES
-    for c in range(chunks):
-        cols = pl.ds(c * LANES, LANES)
-        got = sum(mm(left, piece, NT) for piece in parts(geno[0, cols, :]))
-        payload[pl.ds(c, LANES, stride=rows), :] = got[:LANES]
-        payload[pl.ds(chunks + c, LANES, stride=rows), :] = got[LANES:base]
-        gram = got[base:] - sum(mm(mcf_left, piece, NT) for piece in parts(mg[0, cols, :]))
-        gram = gram[:16] + gram[16:32] + gram[32:48]
-        gram = gram[:K] + first * chunk_of(prod_first, c)
-        out = -first * chunk_of(mw, c)
-        for k in range(K):
-            out = out + table[:, k : k + 1] * gram[k : k + 1, :]
-        weight[pl.ds(c * K, K), :] = out
+    for pair in range(chunks // 2):
+        cols = pl.ds(pair * base, base)
+        got = sum(mm(left, piece, NT) for piece in halves(geno[0, cols, :]))
+        masked = sum(mm(mcf_left, piece, NT) for piece in halves(mg[0, cols, :]))
+        grams = got[base:] - masked
+        grams = grams[:16] + grams[16:32] + grams[32:48]
+        for part in range(2):
+            c = 2 * pair + part
+            lanes = slice(part * LANES, (part + 1) * LANES)
+            payload[pl.ds(c, LANES, stride=rows), :] = got[:LANES, lanes]
+            payload[pl.ds(chunks + c, LANES, stride=rows), :] = got[LANES:base, lanes]
+            gram = grams[:K, lanes] + first * chunk_of(prod_first, c)
+            out = -first * chunk_of(mw, c)
+            for k in range(K):
+                out = out + table[:, k : k + 1] * gram[k : k + 1, :]
+            weight[pl.ds(c * K, K), :] = out
     side = jnp.concatenate(
         [cov_sum, spot.astype(jnp.float32), jnp.zeros((64 - K - 1, width), jnp.float32)], axis=0
     )
@@ -127,7 +135,10 @@
         a_s[0:K, pl.ds(c * LANES, LANES)] = chunk_of(mw, c)
         a_s[16 : 16 + K, pl.ds(c * LANES, LANES)] = ow[c * K : (c + 1) * K]
     spots = jnp.concatenate(place, axis=0)
-    b_all = b_s[...]
+    a_high, a_mid, a_low = parts(a_s[...])
+    b_high, b_mid, b_low = parts(b_s[...])
+    a_all = jnp.concatenate([a_high, a_high, a_high, a_mid, a_mid, a_low], axis=0)
+    b_all = jnp.concatenate([b_high, b_mid, b_low, b_high, b_mid, b_high], axis=0)
     for c in range(chunks):
         cols = pl.ds(c * LANES, LANES)
         sent = jnp.concatenate(
@@ -137,10 +148,8 @@
             ],
             axis=0,
         )
-        geno = sum(mm(piece, spots, TN) for piece in parts(sent))
-        fitted = prod_second[0, cols, :] + lax.dot_general(
-            a_s[:, cols], b_all, TN, precision=HIGH, preferred_element_type=jnp.float32
-        )
+        geno = sum(mm(piece, spots, TN) for piece in halves(sent))
+        fitted = prod_second[0, cols, :] + mm(a_all[:, c * LANES : (c + 1) * LANES], b_all, TN)
         residual = geno - fitted
         for t in range(LANES // 8):
             payload[pl.ds((c * (LANES // 8) + t) * out_rows, 8), :] = residual[8 * t : 8 * t + 8]
@@ -148,21 +157,26 @@
     group = LANES // PHEN
     wide = phen[...]
     blank = jnp.zeros_like(wide)
-    shifted = [
-        jnp.concatenate([wide if g == at else blank for at in range(group)], axis=0)
-        for g in range(group)
-    ]
+    spread = jnp.concatenate(
+        [
+            jnp.concatenate([wide if g == at else blank for at in range(group)], axis=0)
+            for g in range(group)
+        ],
+        axis=1,
+    )
+    p_high, p_mid = halves(spread)
     for half in range(8 // group):
-        total = jnp.zeros((owners, LANES), jnp.float32)
-        for g in range(group):
-            total = total + lax.dot_general(
-                payload[pl.ds(half * group + g, owners, stride=out_rows), :],
-                shifted[g],
-                NT,
-                precision=HIGH,
-                preferred_element_type=jnp.float32,
-            )
-        payload[pl.ds(8 + half, owners, stride=out_rows), :] = total
+        values = jnp.concatenate(
+            [
+                payload[pl.ds(half * group + g, owners, stride=out_rows), :]
+                for g in range(group)
+            ],
+            axis=1,
+        )
+        r_high, r_mid = halves(values)
+        payload[pl.ds(8 + half, owners, stride=out_rows), :] = (
+            mm(r_high, p_mid, NT) + mm(r_mid, p_high, NT) + mm(r_high, p_high, NT)
+        )
 
 
 def finish_kernel(scale, recv, columns, score):

time: 109 us -> 108 us (level)
  Pallas kernels: 7.21 us -> 5.41 us
where the time goes in v1:
time: 108 us; the launch traced here: 107 us
  waiting for transfers between devices  37.6 us (35%)
  starting transfers between devices  36.8 us (34%)
  blocking collectives  26.6 us (25%)
  Pallas kernels  5.41 us (5%)
    all_to_all x1, blocking collectives, exchange(): got = lax.all_to_all(flat, 'smp', split_axis=0, concat_axis=0, tiled=True)  26.6 us
    ppermute x1, waiting for transfers between devices, z_pair(): lax.ppermute(value, 'smp', [(i, i ^ 4) for i in range(lax.axis_size('smp'...  24.5 us
    ppermute x9, starting transfers between devices, shifted(): return lax.ppermute(value, 'smp', pairs)  19.6 us
    all_to_all x1, starting transfers between devices, exchange(): got = lax.all_to_all(flat, 'smp', split_axis=0, concat_axis=0, tiled=True)  15.1 us
    ppermute x9, waiting for transfers between devices, shifted(): return lax.ppermute(value, 'smp', pairs)  11.2 us
    pallas_call x1, Pallas kernels, local(): pl.pallas_call(pack_kernel, out_shape=(jax.ShapeDtypeStruct((peers * (2 *...  3.38 us
  transfers between devices with their start and end apart: 15, of which 11 were waited for; matrix products, arithmetic and copies ran while one was open for 0% of the time, Pallas kernels for 0%

profile of v1, /device:TPU:32, one launch (start us, length us, event | category | flops | bytes accessed | tf_op | source)
XLA Modules:
  0.0 107.3 jit_solution(18368482228222576368)
XLA Ops:
  0.6 0.1 collective-permute-start
  0.7 0.5 collective-permute-start.1
  1.2 1.2 %collective-permute-done.1.mcf_peer = f32[10,1,128]{2,1,0:T(1,128)} collective-permute-done((f32[10,1,128]{2,1,0:T(1,128)}, f32[10,1,128]{2,1,0:T(1,128)}, u32[]{:S(2)}, u32[]{:S(2)}) %collective-permute-start.1) | collective-permute-done | bytes 5152 | tf_op jit(solution)/shard_map/ppermute | solution.py:196
  2.4 3.4 %shard_map.122 = (f32[2176,128]{1,0:T(8,128)}, f32[80,128]{1,0:T(8,128)}) custom-call(s32[1,256]{1,0:T(1,128)} %bitcast.25, f32[1,1024,256]{2,1,0:T(8,128)} %geno.1, f32[10,1,256]{2,1,0:T(1,128)} %bitcast.22, f32[10,1,256]{2,1,0:T(1,128)} %collective-permute-done.cov_peer, f32[10,1,128]{2,1,0:T(1,128)} %bitcast.24, ...), custom_call_target="tpu_custom_call" | custom-call | tf_op jit(solution)/shard_map/pallas_call | solution.py:257
  5.8 0.0 copy-start
  5.8 0.0 copy-start.1
  5.8 0.0 copy-start.2
  5.8 15.1 %all-to-all-start = ((f32[128,1,2176]{2,1,0:T(1,128)}), f32[128,1,2176]{2,1,0:T(1,128)S(1)}, u32[]{:S(2)}, u32[]{:S(2)}) async-start(f32[128,1,2176]{2,1,0:T(1,128)} %bitcast.19), calls=%async_computation | async-start | bytes 2228224 | tf_op jit(solution)/shard_map/all_to_all | solution.py:232
  21.0 1.0 collective-permute-start.2
  22.0 24.5 %collective-permute-done.2 = f32[80,128]{1,0:T(8,128)S(1)} collective-permute-done((f32[80,128]{1,0:T(8,128)S(1)}, f32[80,128]{1,0:T(8,128)S(1)}, u32[]{:S(2)}, u32[]{:S(2)}) %collective-permute-start.2) | collective-permute-done | bytes 40992 | tf_op jit(solution)/shard_map/ppermute | solution.py:214
  46.5 0.5 collective-permute-start.4
  46.9 0.7 collective-permute-done.3
  47.7 0.1 collective-permute-done.4.mcs_peer
  47.8 2.1 %collective-permute-start.7 = (f32[80,128]{1,0:T(8,128)S(1)}, f32[80,128]{1,0:T(8,128)S(1)}, u32[]{:S(2)}, u32[]{:S(2)}) collective-permute-start(f32[80,128]{1,0:T(8,128)S(1)} %add.25), channel_id=1, source_target_pairs={{0,2},{1,3},{2,0},{3,1},{4,6},{5,7},{6,4},{7,5},{8,10},{9,11},{10,... | collective-permute-start | bytes 122888 | tf_op jit(solution)/shard_map/ppermute | solution.py:210
  49.8 1.5 %collective-permute-start.6 = (f32[80,128]{1,0:T(8,128)S(1)}, f32[80,128]{1,0:T(8,128)S(1)}, u32[]{:S(2)}, u32[]{:S(2)}) collective-permute-start(f32[80,128]{1,0:T(8,128)S(1)} %add.25), channel_id=1, source_target_pairs={{0,3},{1,0},{2,1},{3,2},{4,7},{5,4},{6,5},{7,6},{8,11},{9,8},{10,9... | collective-permute-start | bytes 122888 | tf_op jit(solution)/shard_map/ppermute | solution.py:210
  51.3 0.6 collective-permute-start.5
  51.9 1.4 %collective-permute-done.7 = f32[80,128]{1,0:T(8,128)S(1)} collective-permute-done((f32[80,128]{1,0:T(8,128)S(1)}, f32[80,128]{1,0:T(8,128)S(1)}, u32[]{:S(2)}, u32[]{:S(2)}) %collective-permute-start.7) | collective-permute-done | bytes 40992 | tf_op jit(solution)/shard_map/ppermute | solution.py:210
  53.3 0.6 collective-permute-done.6
  53.8 2.7 %collective-permute-done.5 = f32[80,128]{1,0:T(8,128)S(1)} collective-permute-done((f32[80,128]{1,0:T(8,128)S(1)}, f32[80,128]{1,0:T(8,128)S(1)}, u32[]{:S(2)}, u32[]{:S(2)}) %collective-permute-start.5) | collective-permute-done | bytes 40992 | tf_op jit(solution)/shard_map/ppermute | solution.py:210
  56.5 3.3 %collective-permute-start.10 = (f32[80,128]{1,0:T(8,128)S(1)}, f32[80,128]{1,0:T(8,128)S(1)}, u32[]{:S(2)}, u32[]{:S(2)}) collective-permute-start(f32[80,128]{1,0:T(8,128)S(1)} %add_add_fusion.1), channel_id=1, source_target_pairs={{0,64},{1,65},{2,66},{3,67},{4,68},{5,69},{6,70},{7,71},{8,72},{9,... | collective-permute-start | bytes 122888 | tf_op jit(solution)/shard_map/ppermute | solution.py:210
  59.8 0.9 collective-permute-start.9
  60.8 1.1 %collective-permute-start.8 = (f32[80,128]{1,0:T(8,128)S(1)}, f32[80,128]{1,0:T(8,128)S(1)}, u32[]{:S(2)}, u32[]{:S(2)}) collective-permute-start(f32[80,128]{1,0:T(8,128)S(1)} %add_add_fusion.1), channel_id=1, source_target_pairs={{0,32},{1,33},{2,34},{3,35},{4,36},{5,37},{6,38},{7,39},{8,40},{9,... | collective-permute-start | bytes 122888 | tf_op jit(solution)/shard_map/ppermute | solution.py:210
  61.8 0.6 collective-permute-done.10
  62.5 1.4 %collective-permute-done.9 = f32[80,128]{1,0:T(8,128)S(1)} collective-permute-done((f32[80,128]{1,0:T(8,128)S(1)}, f32[80,128]{1,0:T(8,128)S(1)}, u32[]{:S(2)}, u32[]{:S(2)}) %collective-permute-start.9) | collective-permute-done | bytes 40992 | tf_op jit(solution)/shard_map/ppermute | solution.py:210
  63.8 2.2 %collective-permute-done.8 = f32[80,128]{1,0:T(8,128)S(1)} collective-permute-done((f32[80,128]{1,0:T(8,128)S(1)}, f32[80,128]{1,0:T(8,128)S(1)}, u32[]{:S(2)}, u32[]{:S(2)}) %collective-permute-start.8) | collective-permute-done | bytes 40992 | tf_op jit(solution)/shard_map/ppermute | solution.py:210
  66.0 3.0 %collective-permute-start.11 = (f32[80,128]{1,0:T(8,128)S(1)}, f32[80,128]{1,0:T(8,128)S(1)}, u32[]{:S(2)}, u32[]{:S(2)}) collective-permute-start(f32[80,128]{1,0:T(8,128)S(1)} %add_add_fusion.w_0), channel_id=1, source_target_pairs={{0,8},{1,9},{2,10},{3,11},{4,12},{5,13},{6,14},{7,15},{8,16},{9,17... | collective-permute-start | bytes 122888 | tf_op jit(solution)/shard_map/ppermute | solution.py:210
  69.0 1.3 %collective-permute-start.12 = (f32[80,128]{1,0:T(8,128)S(1)}, f32[80,128]{1,0:T(8,128)S(1)}, u32[]{:S(2)}, u32[]{:S(2)}) collective-permute-start(f32[80,128]{1,0:T(8,128)S(1)} %add_add_fusion.w_0), channel_id=1, source_target_pairs={{0,24},{1,25},{2,26},{3,27},{4,28},{5,29},{6,30},{7,31},{8,0},{9,1... | collective-permute-start | bytes 122888 | tf_op jit(solution)/shard_map/ppermute | solution.py:210
  70.2 6.0 %collective-permute-start.13 = (f32[80,128]{1,0:T(8,128)S(1)}, f32[80,128]{1,0:T(8,128)S(1)}, u32[]{:S(2)}, u32[]{:S(2)}) collective-permute-start(f32[80,128]{1,0:T(8,128)S(1)} %add_add_fusion.w_0), channel_id=1, source_target_pairs={{0,16},{1,17},{2,18},{3,19},{4,20},{5,21},{6,22},{7,23},{8,24},{9,... | collective-permute-start | bytes 122888 | tf_op jit(solution)/shard_map/ppermute | solution.py:210
  76.2 2.4 %collective-permute-done.13.w_3 = f32[80,128]{1,0:T(8,128)S(1)} collective-permute-done((f32[80,128]{1,0:T(8,128)S(1)}, f32[80,128]{1,0:T(8,128)S(1)}, u32[]{:S(2)}, u32[]{:S(2)}) %collective-permute-start.13) | collective-permute-done | bytes 40992 | tf_op jit(solution)/shard_map/ppermute | solution.py:210
  78.6 1.2 %shard_map.123 = f32[1280,128]{1,0:T(8,128)S(1)} custom-call(f32[2176,128]{1,0:T(8,128)S(1)} %bitcast.11, f32[80,128]{1,0:T(8,128)S(1)} %add_add_fusion.w_0, f32[80,128]{1,0:T(8,128)S(1)} %collective-permute-done.11.w_1, f32[80,128]{1,0:T(8,128)S(1)} %collective-permute-done.12.w_2, f32[80,128]{1,0:T(8,128)S(1)} %collective-permute-done.13.w_3, ...), custom_call_target="tpu_custom_call" | custom-call | tf_op jit(solution)/shard_map/pallas_call | solution.py:287
  79.8 26.6 %all_to_all.10 = f32[128,1,1280]{2,1,0:T(1,128)S(1)} all-to-all(f32[128,1,1280]{2,1,0:T(1,128)S(1)} %bitcast.13), channel_id=1, replica_groups=mesh['srv'=2,'smp'=128] {'smp'}, dimensions={0} | all-to-all | bytes 1310720 | tf_op jit(solution)/shard_map/all_to_all | solution.py:232
  106.4 0.8 shard_map.124
  (16 shorter events, 0.1 us)
Async XLA Ops:
  0.6 1.8 %collective-permute-start = (f32[10,1,256]{2,1,0:T(1,128)}, f32[10,1,256]{2,1,0:T(1,128)}, u32[]{:S(2)}, u32[]{:S(2)}) collective-permute-start(f32[10,1,256]{2,1,0:T(1,128)} %bitcast.21), channel_id=1, source_target_pairs={{0,128},{128,0},{1,129},{129,1},{2,130},{130,2},{3,131},{131,3},{4... | collective-permute-start | bytes 30728 | tf_op jit(solution)/shard_map/ppermute | solution.py:196
  0.7 1.7 %collective-permute-start.1 = (f32[10,1,128]{2,1,0:T(1,128)}, f32[10,1,128]{2,1,0:T(1,128)}, u32[]{:S(2)}, u32[]{:S(2)}) collective-permute-start(f32[10,1,128]{2,1,0:T(1,128)} %bitcast.23), channel_id=1, source_target_pairs={{0,128},{128,0},{1,129},{129,1},{2,130},{130,2},{3,131},{131,3},{4... | collective-permute-start | bytes 15368 | tf_op jit(solution)/shard_map/ppermute | solution.py:196
  5.8 15.2 %copy-start.4 = (f32[80,128]{1,0:T(8,128)S(1)}, f32[80,128]{1,0:T(8,128)}, u32[]{:S(2)}) copy-start(f32[80,128]{1,0:T(8,128)} %get-tuple-element.7) | copy-start | bytes 122884
  5.8 40.7 %copy-start.3 = (f32[1,10,128]{2,0,1:T(1,128)S(1)}, f32[1,10,128]{2,0,1:T(1,128)}, u32[]{:S(2)}) copy-start(f32[1,10,128]{2,0,1:T(1,128)} %param.17) | copy-start | bytes 15364
  5.8 72.8 %copy-start = (f32[1,1024,128]{2,1,0:T(8,128)S(1)}, f32[1,1024,128]{2,1,0:T(8,128)}, u32[]{:S(2)}) copy-start(f32[1,1024,128]{2,1,0:T(8,128)} %prod_second.1) | copy-start | bytes 1572868
  5.8 72.8 %copy-start.1 = (f32[1,10,1024]{2,0,1:T(1,128)S(1)}, f32[1,10,1024]{2,0,1:T(1,128)}, u32[]{:S(2)}) copy-start(f32[1,10,1024]{2,0,1:T(1,128)} %param.18) | copy-start | bytes 122884
  5.8 72.8 %copy-start.2 = (f32[128,32]{0,1:T(8,128)S(1)}, f32[128,32]{0,1:T(8,128)}, u32[]{:S(2)}) copy-start(f32[128,32]{0,1:T(8,128)} %param.21) | copy-start | bytes 49156
  5.8 72.8 %all-to-all-start = ((f32[128,1,2176]{2,1,0:T(1,128)}), f32[128,1,2176]{2,1,0:T(1,128)S(1)}, u32[]{:S(2)}, u32[]{:S(2)}) async-start(f32[128,1,2176]{2,1,0:T(1,128)} %bitcast.19), calls=%async_computation | async-start | bytes 2228224 | tf_op jit(solution)/shard_map/all_to_all | solution.py:232
  21.0 25.4 %collective-permute-start.2 = (f32[80,128]{1,0:T(8,128)S(1)}, f32[80,128]{1,0:T(8,128)S(1)}, u32[]{:S(2)}, u32[]{:S(2)}) collective-permute-start(f32[80,128]{1,0:T(8,128)S(1)} %copy-done.4), channel_id=1, source_target_pairs={{0,4},{1,5},{2,6},{3,7},{4,0},{5,1},{6,2},{7,3},{8,12},{9,13},{10,... | collective-permute-start | bytes 122888 | tf_op jit(solution)/shard_map/ppermute | solution.py:214
  46.4 1.2 %collective-permute-start.3 = (f32[80,128]{1,0:T(8,128)S(1)}, f32[80,128]{1,0:T(8,128)S(1)}, u32[]{:S(2)}, u32[]{:S(2)}) collective-permute-start(f32[80,128]{1,0:T(8,128)S(1)} %add.24), channel_id=1, source_target_pairs={{0,128},{128,0},{1,129},{129,1},{2,130},{130,2},{3,131},{131,3},{4... | collective-permute-start | bytes 122888 | tf_op jit(solution)/shard_map/ppermute | solution.py:196
  46.5 1.3 %collective-permute-start.4 = (f32[10,1,128]{2,1,0:T(1,128)S(1)}, f32[10,1,128]{2,1,0:T(1,128)S(1)}, u32[]{:S(2)}, u32[]{:S(2)}) collective-permute-start(f32[10,1,128]{2,1,0:T(1,128)S(1)} %bitcast.17), channel_id=1, source_target_pairs={{0,128},{128,0},{1,129},{129,1},{2,130},{130,2},{3,131},{131,3},{4... | collective-permute-start | bytes 15368 | tf_op jit(solution)/shard_map/ppermute | solution.py:196
  47.8 5.5 %collective-permute-start.7 = (f32[80,128]{1,0:T(8,128)S(1)}, f32[80,128]{1,0:T(8,128)S(1)}, u32[]{:S(2)}, u32[]{:S(2)}) collective-permute-start(f32[80,128]{1,0:T(8,128)S(1)} %add.25), channel_id=1, source_target_pairs={{0,2},{1,3},{2,0},{3,1},{4,6},{5,7},{6,4},{7,5},{8,10},{9,11},{10,... | collective-permute-start | bytes 122888 | tf_op jit(solution)/shard_map/ppermute | solution.py:210
  49.8 4.0 %collective-permute-start.6 = (f32[80,128]{1,0:T(8,128)S(1)}, f32[80,128]{1,0:T(8,128)S(1)}, u32[]{:S(2)}, u32[]{:S(2)}) collective-permute-start(f32[80,128]{1,0:T(8,128)S(1)} %add.25), channel_id=1, source_target_pairs={{0,3},{1,0},{2,1},{3,2},{4,7},{5,4},{6,5},{7,6},{8,11},{9,8},{10,9... | collective-permute-start | bytes 122888 | tf_op jit(solution)/shard_map/ppermute | solution.py:210
  51.3 5.2 %collective-permute-start.5 = (f32[80,128]{1,0:T(8,128)S(1)}, f32[80,128]{1,0:T(8,128)S(1)}, u32[]{:S(2)}, u32[]{:S(2)}) collective-permute-start(f32[80,128]{1,0:T(8,128)S(1)} %add.25), channel_id=1, source_target_pairs={{0,1},{1,2},{2,3},{3,0},{4,5},{5,6},{6,7},{7,4},{8,9},{9,10},{10,1... | collective-permute-start | bytes 122888 | tf_op jit(solution)/shard_map/ppermute | solution.py:210
  56.5 5.9 %collective-permute-start.10 = (f32[80,128]{1,0:T(8,128)S(1)}, f32[80,128]{1,0:T(8,128)S(1)}, u32[]{:S(2)}, u32[]{:S(2)}) collective-permute-start(f32[80,128]{1,0:T(8,128)S(1)} %add_add_fusion.1), channel_id=1, source_target_pairs={{0,64},{1,65},{2,66},{3,67},{4,68},{5,69},{6,70},{7,71},{8,72},{9,... | collective-permute-start | bytes 122888 | tf_op jit(solution)/shard_map/ppermute | solution.py:210
  59.8 4.0 %collective-permute-start.9 = (f32[80,128]{1,0:T(8,128)S(1)}, f32[80,128]{1,0:T(8,128)S(1)}, u32[]{:S(2)}, u32[]{:S(2)}) collective-permute-start(f32[80,128]{1,0:T(8,128)S(1)} %add_add_fusion.1), channel_id=1, source_target_pairs={{0,96},{1,97},{2,98},{3,99},{4,100},{5,101},{6,102},{7,103},{8,104... | collective-permute-start | bytes 122888 | tf_op jit(solution)/shard_map/ppermute | solution.py:210
  60.8 5.2 %collective-permute-start.8 = (f32[80,128]{1,0:T(8,128)S(1)}, f32[80,128]{1,0:T(8,128)S(1)}, u32[]{:S(2)}, u32[]{:S(2)}) collective-permute-start(f32[80,128]{1,0:T(8,128)S(1)} %add_add_fusion.1), channel_id=1, source_target_pairs={{0,32},{1,33},{2,34},{3,35},{4,36},{5,37},{6,38},{7,39},{8,40},{9,... | collective-permute-start | bytes 122888 | tf_op jit(solution)/shard_map/ppermute | solution.py:210
  66.0 10.2 %collective-permute-start.11 = (f32[80,128]{1,0:T(8,128)S(1)}, f32[80,128]{1,0:T(8,128)S(1)}, u32[]{:S(2)}, u32[]{:S(2)}) collective-permute-start(f32[80,128]{1,0:T(8,128)S(1)} %add_add_fusion.w_0), channel_id=1, source_target_pairs={{0,8},{1,9},{2,10},{3,11},{4,12},{5,13},{6,14},{7,15},{8,16},{9,17... | collective-permute-start | bytes 122888 | tf_op jit(solution)/shard_map/ppermute | solution.py:210
  69.0 7.2 %collective-permute-start.12 = (f32[80,128]{1,0:T(8,128)S(1)}, f32[80,128]{1,0:T(8,128)S(1)}, u32[]{:S(2)}, u32[]{:S(2)}) collective-permute-start(f32[80,128]{1,0:T(8,128)S(1)} %add_add_fusion.w_0), channel_id=1, source_target_pairs={{0,24},{1,25},{2,26},{3,27},{4,28},{5,29},{6,30},{7,31},{8,0},{9,1... | collective-permute-start | bytes 122888 | tf_op jit(solution)/shard_map/ppermute | solution.py:210
  70.2 8.4 %collective-permute-start.13 = (f32[80,128]{1,0:T(8,128)S(1)}, f32[80,128]{1,0:T(8,128)S(1)}, u32[]{:S(2)}, u32[]{:S(2)}) collective-permute-start(f32[80,128]{1,0:T(8,128)S(1)} %add_add_fusion.w_0), channel_id=1, source_target_pairs={{0,16},{1,17},{2,18},{3,19},{4,20},{5,21},{6,22},{7,23},{8,24},{9,... | collective-permute-start | bytes 122888 | tf_op jit(solution)/shard_map/ppermute | solution.py:210

commit v2 on v1

--- a/solution.py
+++ b/solution.py
@@ -14,6 +14,8 @@
 NT = (((1,), (1,)), ((), ()))
 TN = (((0,), (0,)), ((), ()))
 VMEM = pl.BlockSpec(memory_space=pltpu.VMEM)
+ANY = pl.BlockSpec(memory_space=pltpu.HBM)
+OUT = pl.BlockSpec(memory_space=pl.ANY)
 TIGHT = pltpu.CompilerParams(vmem_limit_bytes=67043328)
 ROOM = pltpu.CompilerParams(vmem_limit_bytes=16 << 20)
 
@@ -45,6 +47,29 @@
 
 def plain(ref):
     return jnp.concatenate([ref[k] for k in range(ref.shape[0])], axis=0)
+
+
+def fetch_kernel(*refs):
+    count = (len(refs) - 1) // 2
+    sems = refs[-1]
+    copies = [
+        pltpu.make_async_copy(refs[n], refs[count + n], sems.at[n]) for n in range(count)
+    ]
+    for copy in copies:
+        copy.start()
+    for copy in copies:
+        copy.wait()
+
+
+def fetch(*arrays):
+    return pl.pallas_call(
+        fetch_kernel,
+        out_shape=tuple(jax.ShapeDtypeStruct(array.shape, array.dtype) for array in arrays),
+        in_specs=[ANY] * len(arrays),
+        out_specs=tuple(OUT for array in arrays),
+        scratch_shapes=[pltpu.SemaphoreType.DMA((len(arrays),))],
+        compiler_params=ROOM,
+    )(*[pltpu.with_memory_space_constraint(array, pltpu.HBM) for array in arrays])
 
 
 def pack_kernel(
@@ -254,6 +279,9 @@
     )
     cov_peer, mcf_peer = swap((cov, mcf))
     first_product, mw = (rows_of(value.transpose(1, 0, 2)) for value in (prod_first, mask_weight))
+    ids, geno, near_cov, near_mcf, mg, near_first, near_mw, table = fetch(
+        sample_ids[None], genotype_sites, cov, mcf, mask_geno, first_product, mw, coef
+    )
     packed, weight = pl.pallas_call(
         pack_kernel,
         out_shape=(
@@ -262,19 +290,8 @@
         ),
         in_specs=[VMEM] * 10,
         out_specs=(VMEM, VMEM),
-        compiler_params=TIGHT,
-    )(
-        sample_ids[None],
-        genotype_sites,
-        cov,
-        cov_peer,
-        mcf,
-        mcf_peer,
-        mask_geno,
-        first_product,
-        mw,
-        coef,
-    )
+        compiler_params=ROOM,
+    )(ids, geno, near_cov, cov_peer, near_mcf, mcf_peer, mg, near_first, near_mw, table)
     received = exchange(packed, peers)
     other = z_pair(weight)
     weight = weight + other

time: 108 us -> 108 us (level)
  waiting for transfers between devices: 37.6 us -> 34 us
  blocking collectives: 26.6 us -> 30.1 us
    all_to_all x1, blocking collectives: 26.6 us -> 30.1 us  [exchange(): got = lax.all_to_all(flat, 'smp', split_axis=0, concat_axis=0, tiled=True)]
    ppermute x9, waiting for transfers between devices: 11.2 us -> 8.97 us  [shifted(): return lax.ppermute(value, 'smp', pairs)]
    pallas_call x0 -> x1, Pallas kernels: none -> 1.48 us  [fetch(): pl.pallas_call(fetch_kernel, out_shape=tuple((jax.ShapeDtypeStruct(array....]
    pallas_call x1, Pallas kernels: 3.38 us -> 1.93 us  [local(): pl.pallas_call(pack_kernel, out_shape=(jax.ShapeDtypeStruct((peers * (2 *...]
    ppermute x4, waiting for transfers between devices: 1.99 us -> 0.82 us  [swap(): return lax.ppermute(value, 'srv', [(0, 1), (1, 0)])]
  transfers between devices with their start and end apart: 15 -> 15, of which waited for: 11 -> 7; matrix products, arithmetic and copies ran while one was open for 0% -> 0% of each run, Pallas kernels for 0% -> 1%
where the time goes in v2:
time: 108 us
  starting transfers between devices  37.5 us (35%)
  waiting for transfers between devices  34 us (31%)
  blocking collectives  30.1 us (28%)
  Pallas kernels  5.46 us (5%)
    all_to_all x1, blocking collectives, exchange(): got = lax.all_to_all(flat, 'smp', split_axis=0, concat_axis=0, tiled=True)  30.1 us
    ppermute x1, waiting for transfers between devices, z_pair(): lax.ppermute(value, 'smp', [(i, i ^ 4) for i in range(lax.axis_size('smp'...  24.2 us
    ppermute x9, starting transfers between devices, shifted(): return lax.ppermute(value, 'smp', pairs)  20.3 us
    all_to_all x1, starting transfers between devices, exchange(): got = lax.all_to_all(flat, 'smp', split_axis=0, concat_axis=0, tiled=True)  15.1 us
    ppermute x9, waiting for transfers between devices, shifted(): return lax.ppermute(value, 'smp', pairs)  8.97 us
  transfers between devices with their start and end apart: 15, of which 7 were waited for; matrix products, arithmetic and copies ran while one was open for 0% of the time, Pallas kernels for 1%

profile of v2, /device:TPU:32, one launch (start us, length us, event | category | flops | bytes accessed | tf_op | source)
XLA Modules:
  0.0 107.8 jit_solution(10546885248122477404)
XLA Ops:
  0.6 0.1 collective-permute-start
  0.7 0.5 collective-permute-start.1
  1.2 1.5 %shard_map.122 = (s32[1,256]{1,0:T(1,128)S(1)}, f32[1,1024,256]{2,1,0:T(8,128)S(1)}, f32[10,1,256]{2,1,0:T(1,128)S(1)}, f32[10,1,128]{2,1,0:T(1,128)S(1)}, f32[1...) custom-call(s32[1,256]{1,0:T(1,128)} %bitcast.24, ...), custom_call_target="tpu_custom_call" | custom-call | tf_op jit(solution)/shard_map/pallas_call | solution.py:65
  2.7 0.0 collective-permute-done.1.mcf_peer
  2.7 0.0 collective-permute-done.cov_peer
  2.7 1.9 %shard_map.123 = (f32[2176,128]{1,0:T(8,128)}, f32[80,128]{1,0:T(8,128)S(1)}) custom-call(s32[1,256]{1,0:T(1,128)S(1)} %get-tuple-element.14.ids, f32[1,1024,256]{2,1,0:T(8,128)S(1)} %get-tuple-element.15.geno, f32[10,1,256]{2,1,0:T(1,128)S(1)} %get-tuple-element.16.cov, f32[10,1,256]{2,1,0:T(1,128)S(1)} %collective-permute-done.cov_peer, ...), custom_call_target="tpu_custom_call" | custom-call | tf_op jit(solution)/shard_map/pallas_call | solution.py:285
  4.7 15.1 %all-to-all-start = ((f32[128,1,2176]{2,1,0:T(1,128)}), f32[128,1,2176]{2,1,0:T(1,128)S(1)}, u32[]{:S(2)}, u32[]{:S(2)}) async-start(f32[128,1,2176]{2,1,0:T(1,128)} %bitcast.5), calls=%async_computation | async-start | bytes 2228224 | tf_op jit(solution)/shard_map/all_to_all | solution.py:257
  19.8 1.0 collective-permute-start.2
  20.8 24.2 %collective-permute-done.2 = f32[80,128]{1,0:T(8,128)S(1)} collective-permute-done((f32[80,128]{1,0:T(8,128)S(1)}, f32[80,128]{1,0:T(8,128)S(1)}, u32[]{:S(2)}, u32[]{:S(2)}) %collective-permute-start.2) | collective-permute-done | bytes 40992 | tf_op jit(solution)/shard_map/ppermute | solution.py:239
  45.0 0.0 collective-permute-start.3
  45.1 0.5 collective-permute-start.4
  45.6 0.7 collective-permute-done.3
  46.3 0.1 collective-permute-done.4.mcs_peer
  46.4 0.8 collective-permute-start.5
  47.2 2.4 %collective-permute-start.6 = (f32[80,128]{1,0:T(8,128)S(1)}, f32[80,128]{1,0:T(8,128)S(1)}, u32[]{:S(2)}, u32[]{:S(2)}) collective-permute-start(f32[80,128]{1,0:T(8,128)S(1)} %add.25), channel_id=1, source_target_pairs={{0,3},{1,0},{2,1},{3,2},{4,7},{5,4},{6,5},{7,6},{8,11},{9,8},{10,9... | collective-permute-start | bytes 122888 | tf_op jit(solution)/shard_map/ppermute | solution.py:235
  49.6 0.9 collective-permute-start.7
  50.5 1.1 collective-permute-done.5
  51.6 3.5 %collective-permute-done.7 = f32[80,128]{1,0:T(8,128)S(1)} collective-permute-done((f32[80,128]{1,0:T(8,128)S(1)}, f32[80,128]{1,0:T(8,128)S(1)}, u32[]{:S(2)}, u32[]{:S(2)}) %collective-permute-start.7) | collective-permute-done | bytes 40992 | tf_op jit(solution)/shard_map/ppermute | solution.py:235
  55.1 2.4 %collective-permute-start.10 = (f32[80,128]{1,0:T(8,128)S(1)}, f32[80,128]{1,0:T(8,128)S(1)}, u32[]{:S(2)}, u32[]{:S(2)}) collective-permute-start(f32[80,128]{1,0:T(8,128)S(1)} %add_add_fusion.1), channel_id=1, source_target_pairs={{0,64},{1,65},{2,66},{3,67},{4,68},{5,69},{6,70},{7,71},{8,72},{9,... | collective-permute-start | bytes 122888 | tf_op jit(solution)/shard_map/ppermute | solution.py:235
  57.6 0.8 collective-permute-start.8
  58.4 2.5 %collective-permute-start.9 = (f32[80,128]{1,0:T(8,128)S(1)}, f32[80,128]{1,0:T(8,128)S(1)}, u32[]{:S(2)}, u32[]{:S(2)}) collective-permute-start(f32[80,128]{1,0:T(8,128)S(1)} %add_add_fusion.1), channel_id=1, source_target_pairs={{0,96},{1,97},{2,98},{3,99},{4,100},{5,101},{6,102},{7,103},{8,104... | collective-permute-start | bytes 122888 | tf_op jit(solution)/shard_map/ppermute | solution.py:235
  60.8 0.0 collective-permute-done.10
  60.8 2.0 %collective-permute-done.8 = f32[80,128]{1,0:T(8,128)S(1)} collective-permute-done((f32[80,128]{1,0:T(8,128)S(1)}, f32[80,128]{1,0:T(8,128)S(1)}, u32[]{:S(2)}, u32[]{:S(2)}) %collective-permute-start.8) | collective-permute-done | bytes 40992 | tf_op jit(solution)/shard_map/ppermute | solution.py:235
  62.8 3.2 %collective-permute-start.11 = (f32[80,128]{1,0:T(8,128)S(1)}, f32[80,128]{1,0:T(8,128)S(1)}, u32[]{:S(2)}, u32[]{:S(2)}) collective-permute-start(f32[80,128]{1,0:T(8,128)S(1)} %add_add_fusion.w_0), channel_id=1, source_target_pairs={{0,8},{1,9},{2,10},{3,11},{4,12},{5,13},{6,14},{7,15},{8,16},{9,17... | collective-permute-start | bytes 122888 | tf_op jit(solution)/shard_map/ppermute | solution.py:235
  66.0 1.2 %collective-permute-start.12 = (f32[80,128]{1,0:T(8,128)S(1)}, f32[80,128]{1,0:T(8,128)S(1)}, u32[]{:S(2)}, u32[]{:S(2)}) collective-permute-start(f32[80,128]{1,0:T(8,128)S(1)} %add_add_fusion.w_0), channel_id=1, source_target_pairs={{0,24},{1,25},{2,26},{3,27},{4,28},{5,29},{6,30},{7,31},{8,0},{9,1... | collective-permute-start | bytes 122888 | tf_op jit(solution)/shard_map/ppermute | solution.py:235
  67.2 6.1 %collective-permute-start.13 = (f32[80,128]{1,0:T(8,128)S(1)}, f32[80,128]{1,0:T(8,128)S(1)}, u32[]{:S(2)}, u32[]{:S(2)}) collective-permute-start(f32[80,128]{1,0:T(8,128)S(1)} %add_add_fusion.w_0), channel_id=1, source_target_pairs={{0,16},{1,17},{2,18},{3,19},{4,20},{5,21},{6,22},{7,23},{8,24},{9,... | collective-permute-start | bytes 122888 | tf_op jit(solution)/shard_map/ppermute | solution.py:235
  73.3 0.0 collective-permute-done.11.w_1
  73.3 0.0 collective-permute-done.12.w_2
  73.3 2.4 %collective-permute-done.13.w_3 = f32[80,128]{1,0:T(8,128)S(1)} collective-permute-done((f32[80,128]{1,0:T(8,128)S(1)}, f32[80,128]{1,0:T(8,128)S(1)}, u32[]{:S(2)}, u32[]{:S(2)}) %collective-permute-start.13) | collective-permute-done | bytes 40992 | tf_op jit(solution)/shard_map/ppermute | solution.py:235
  75.7 1.2 %shard_map.124 = f32[1280,128]{1,0:T(8,128)S(1)} custom-call(f32[2176,128]{1,0:T(8,128)S(1)} %bitcast.11, f32[80,128]{1,0:T(8,128)S(1)} %add_add_fusion.w_0, f32[80,128]{1,0:T(8,128)S(1)} %collective-permute-done.11.w_1, f32[80,128]{1,0:T(8,128)S(1)} %collective-permute-done.12.w_2, f32[80,128]{1,0:T(8,128)S(1)} %collective-permute-done.13.w_3, ...), custom_call_target="tpu_custom_call" | custom-call | tf_op jit(solution)/shard_map/pallas_call | solution.py:304
  76.9 30.1 %all_to_all.10 = f32[128,1,1280]{2,1,0:T(1,128)S(1)} all-to-all(f32[128,1,1280]{2,1,0:T(1,128)S(1)} %bitcast.13), channel_id=1, replica_groups=mesh['srv'=2,'smp'=128] {'smp'}, dimensions={0} | all-to-all | bytes 1310720 | tf_op jit(solution)/shard_map/all_to_all | solution.py:257
  107.0 0.8 shard_map.125
  (15 shorter events, 0.1 us)
Async XLA Ops:
  0.6 2.1 %collective-permute-start = (f32[10,1,256]{2,1,0:T(1,128)}, f32[10,1,256]{2,1,0:T(1,128)S(1)}, u32[]{:S(2)}, u32[]{:S(2)}) collective-permute-start(f32[10,1,256]{2,1,0:T(1,128)} %bitcast.20), channel_id=1, source_target_pairs={{0,128},{128,0},{1,129},{129,1},{2,130},{130,2},{3,131},{131,3},{4... | collective-permute-start | bytes 30728 | tf_op jit(solution)/shard_map/ppermute | solution.py:221
  0.7 2.0 %collective-permute-start.1 = (f32[10,1,128]{2,1,0:T(1,128)}, f32[10,1,128]{2,1,0:T(1,128)S(1)}, u32[]{:S(2)}, u32[]{:S(2)}) collective-permute-start(f32[10,1,128]{2,1,0:T(1,128)} %bitcast.22), channel_id=1, source_target_pairs={{0,128},{128,0},{1,129},{129,1},{2,130},{130,2},{3,131},{131,3},{4... | collective-permute-start | bytes 15368 | tf_op jit(solution)/shard_map/ppermute | solution.py:221
  4.7 40.4 %copy-start.3 = (f32[1,10,128]{2,0,1:T(1,128)S(1)}, f32[1,10,128]{2,0,1:T(1,128)}, u32[]{:S(2)}) copy-start(f32[1,10,128]{2,0,1:T(1,128)} %param.17) | copy-start | bytes 15364
  4.7 71.0 %copy-start = (f32[1,1024,128]{2,1,0:T(8,128)S(1)}, f32[1,1024,128]{2,1,0:T(8,128)}, u32[]{:S(2)}) copy-start(f32[1,1024,128]{2,1,0:T(8,128)} %prod_second.1) | copy-start | bytes 1572868
  4.7 71.0 %copy-start.1 = (f32[1,10,1024]{2,0,1:T(1,128)S(1)}, f32[1,10,1024]{2,0,1:T(1,128)}, u32[]{:S(2)}) copy-start(f32[1,10,1024]{2,0,1:T(1,128)} %param.18) | copy-start | bytes 122884
  4.7 71.0 %copy-start.2 = (f32[128,32]{0,1:T(8,128)S(1)}, f32[128,32]{0,1:T(8,128)}, u32[]{:S(2)}) copy-start(f32[128,32]{0,1:T(8,128)} %param.21) | copy-start | bytes 49156
  4.7 71.0 %all-to-all-start = ((f32[128,1,2176]{2,1,0:T(1,128)}), f32[128,1,2176]{2,1,0:T(1,128)S(1)}, u32[]{:S(2)}, u32[]{:S(2)}) async-start(f32[128,1,2176]{2,1,0:T(1,128)} %bitcast.5), calls=%async_computation | async-start | bytes 2228224 | tf_op jit(solution)/shard_map/all_to_all | solution.py:257
  19.8 25.2 %collective-permute-start.2 = (f32[80,128]{1,0:T(8,128)S(1)}, f32[80,128]{1,0:T(8,128)S(1)}, u32[]{:S(2)}, u32[]{:S(2)}) collective-permute-start(f32[80,128]{1,0:T(8,128)S(1)} %get-tuple-element.23), channel_id=1, source_target_pairs={{0,4},{1,5},{2,6},{3,7},{4,0},{5,1},{6,2},{7,3},{8,12},{9,13},{10,... | collective-permute-start | bytes 122888 | tf_op jit(solution)/shard_map/ppermute | solution.py:239
  45.0 1.2 %collective-permute-start.3 = (f32[80,128]{1,0:T(8,128)S(1)}, f32[80,128]{1,0:T(8,128)S(1)}, u32[]{:S(2)}, u32[]{:S(2)}) collective-permute-start(f32[80,128]{1,0:T(8,128)S(1)} %add.24), channel_id=1, source_target_pairs={{0,128},{128,0},{1,129},{129,1},{2,130},{130,2},{3,131},{131,3},{4... | collective-permute-start | bytes 122888 | tf_op jit(solution)/shard_map/ppermute | solution.py:221
  45.1 1.3 %collective-permute-start.4 = (f32[10,1,128]{2,1,0:T(1,128)S(1)}, f32[10,1,128]{2,1,0:T(1,128)S(1)}, u32[]{:S(2)}, u32[]{:S(2)}) collective-permute-start(f32[10,1,128]{2,1,0:T(1,128)S(1)} %bitcast.17), channel_id=1, source_target_pairs={{0,128},{128,0},{1,129},{129,1},{2,130},{130,2},{3,131},{131,3},{4... | collective-permute-start | bytes 15368 | tf_op jit(solution)/shard_map/ppermute | solution.py:221
  46.4 5.2 %collective-permute-start.5 = (f32[80,128]{1,0:T(8,128)S(1)}, f32[80,128]{1,0:T(8,128)S(1)}, u32[]{:S(2)}, u32[]{:S(2)}) collective-permute-start(f32[80,128]{1,0:T(8,128)S(1)} %add.25), channel_id=1, source_target_pairs={{0,1},{1,2},{2,3},{3,0},{4,5},{5,6},{6,7},{7,4},{8,9},{9,10},{10,1... | collective-permute-start | bytes 122888 | tf_op jit(solution)/shard_map/ppermute | solution.py:235
  47.2 4.4 %collective-permute-start.6 = (f32[80,128]{1,0:T(8,128)S(1)}, f32[80,128]{1,0:T(8,128)S(1)}, u32[]{:S(2)}, u32[]{:S(2)}) collective-permute-start(f32[80,128]{1,0:T(8,128)S(1)} %add.25), channel_id=1, source_target_pairs={{0,3},{1,0},{2,1},{3,2},{4,7},{5,4},{6,5},{7,6},{8,11},{9,8},{10,9... | collective-permute-start | bytes 122888 | tf_op jit(solution)/shard_map/ppermute | solution.py:235
  49.6 5.5 %collective-permute-start.7 = (f32[80,128]{1,0:T(8,128)S(1)}, f32[80,128]{1,0:T(8,128)S(1)}, u32[]{:S(2)}, u32[]{:S(2)}) collective-permute-start(f32[80,128]{1,0:T(8,128)S(1)} %add.25), channel_id=1, source_target_pairs={{0,2},{1,3},{2,0},{3,1},{4,6},{5,7},{6,4},{7,5},{8,10},{9,11},{10,... | collective-permute-start | bytes 122888 | tf_op jit(solution)/shard_map/ppermute | solution.py:235
  55.1 5.7 %collective-permute-start.10 = (f32[80,128]{1,0:T(8,128)S(1)}, f32[80,128]{1,0:T(8,128)S(1)}, u32[]{:S(2)}, u32[]{:S(2)}) collective-permute-start(f32[80,128]{1,0:T(8,128)S(1)} %add_add_fusion.1), channel_id=1, source_target_pairs={{0,64},{1,65},{2,66},{3,67},{4,68},{5,69},{6,70},{7,71},{8,72},{9,... | collective-permute-start | bytes 122888 | tf_op jit(solution)/shard_map/ppermute | solution.py:235
  57.6 5.2 %collective-permute-start.8 = (f32[80,128]{1,0:T(8,128)S(1)}, f32[80,128]{1,0:T(8,128)S(1)}, u32[]{:S(2)}, u32[]{:S(2)}) collective-permute-start(f32[80,128]{1,0:T(8,128)S(1)} %add_add_fusion.1), channel_id=1, source_target_pairs={{0,32},{1,33},{2,34},{3,35},{4,36},{5,37},{6,38},{7,39},{8,40},{9,... | collective-permute-start | bytes 122888 | tf_op jit(solution)/shard_map/ppermute | solution.py:235
  58.4 4.4 %collective-permute-start.9 = (f32[80,128]{1,0:T(8,128)S(1)}, f32[80,128]{1,0:T(8,128)S(1)}, u32[]{:S(2)}, u32[]{:S(2)}) collective-permute-start(f32[80,128]{1,0:T(8,128)S(1)} %add_add_fusion.1), channel_id=1, source_target_pairs={{0,96},{1,97},{2,98},{3,99},{4,100},{5,101},{6,102},{7,103},{8,104... | collective-permute-start | bytes 122888 | tf_op jit(solution)/shard_map/ppermute | solution.py:235
  62.8 10.5 %collective-permute-start.11 = (f32[80,128]{1,0:T(8,128)S(1)}, f32[80,128]{1,0:T(8,128)S(1)}, u32[]{:S(2)}, u32[]{:S(2)}) collective-permute-start(f32[80,128]{1,0:T(8,128)S(1)} %add_add_fusion.w_0), channel_id=1, source_target_pairs={{0,8},{1,9},{2,10},{3,11},{4,12},{5,13},{6,14},{7,15},{8,16},{9,17... | collective-permute-start | bytes 122888 | tf_op jit(solution)/shard_map/ppermute | solution.py:235
  66.0 7.2 %collective-permute-start.12 = (f32[80,128]{1,0:T(8,128)S(1)}, f32[80,128]{1,0:T(8,128)S(1)}, u32[]{:S(2)}, u32[]{:S(2)}) collective-permute-start(f32[80,128]{1,0:T(8,128)S(1)} %add_add_fusion.w_0), channel_id=1, source_target_pairs={{0,24},{1,25},{2,26},{3,27},{4,28},{5,29},{6,30},{7,31},{8,0},{9,1... | collective-permute-start | bytes 122888 | tf_op jit(solution)/shard_map/ppermute | solution.py:235
  67.2 8.5 %collective-permute-start.13 = (f32[80,128]{1,0:T(8,128)S(1)}, f32[80,128]{1,0:T(8,128)S(1)}, u32[]{:S(2)}, u32[]{:S(2)}) collective-permute-start(f32[80,128]{1,0:T(8,128)S(1)} %add_add_fusion.w_0), channel_id=1, source_target_pairs={{0,16},{1,17},{2,18},{3,19},{4,20},{5,21},{6,22},{7,23},{8,24},{9,... | collective-permute-start | bytes 122888 | tf_op jit(solution)/shard_map/ppermute | solution.py:235

commit v3 on v2

--- a/solution.py
+++ b/solution.py
@@ -235,8 +235,8 @@
     return lax.ppermute(value, "smp", pairs)
 
 
-def z_pair(value):
-    return lax.ppermute(value, "smp", [(i, i ^ 4) for i in range(lax.axis_size("smp"))])
+def z_opposite(value):
+    return shifted(value, 0, 4, 0)
 
 
 def terms(value, *moves):
@@ -293,14 +293,14 @@
         compiler_params=ROOM,
     )(ids, geno, near_cov, cov_peer, near_mcf, mcf_peer, mg, near_first, near_mw, table)
     received = exchange(packed, peers)
-    other = z_pair(weight)
+    other = z_opposite(weight)
     weight = weight + other
     weight = weight + swap(weight)
     mcs_peer = swap(mcs)
     weight, mcs_peer = lax.optimization_barrier((weight, mcs_peer))
     weight = total(terms(weight, (0, 0, 1), (0, 0, 3), (0, 0, 2)))
     weight = total(terms(weight, (1, 0, 0), (3, 0, 0), (2, 0, 0)))
-    open_weight = terms(weight, (0, 2, 0), (0, 6, 0), (0, 4, 0))
+    open_weight = terms(weight, (0, 1, 0), (0, 7, 0), (0, 2, 0))
     fitted = pl.pallas_call(
         fit_kernel,
         out_shape=jax.ShapeDtypeStruct((variants // 8 * 10, LANES), jnp.float32),

time: 108 us -> 106 us (0.981)
  waiting for transfers between devices: 34 us -> 37.9 us
  blocking collectives: 30.1 us -> 27.1 us
  starting transfers between devices: 37.5 us -> 34.6 us
    ppermute x9 -> x10, waiting for transfers between devices: 8.97 us -> 37.1 us  [shifted(): return lax.ppermute(value, 'smp', pairs)]
    ppermute x1 -> x0, waiting for transfers between devices: 24.2 us -> none  [z_pair(): lax.ppermute(value, 'smp', [(i, i ^ 4) for i in range(lax.axis_size('smp'...]
    all_to_all x1, blocking collectives: 30.1 us -> 27.1 us  [exchange(): got = lax.all_to_all(flat, 'smp', split_axis=0, concat_axis=0, tiled=True)]
    ppermute x9 -> x10, starting transfers between devices: 20.3 us -> 18.4 us  [shifted(): return lax.ppermute(value, 'smp', pairs)]
  transfers between devices with their start and end apart: 15 -> 15, of which waited for: 7 -> 9; matrix products, arithmetic and copies ran while one was open for 0% -> 0% of each run, Pallas kernels for 1% -> 1%
where the time goes in v3:
time: 106 us
  waiting for transfers between devices  37.9 us (36%)
  starting transfers between devices  34.6 us (33%)
  blocking collectives  27.1 us (26%)
  Pallas kernels  5.45 us (5%)
    ppermute x10, waiting for transfers between devices, shifted(): return lax.ppermute(value, 'smp', pairs)  37.1 us
    all_to_all x1, blocking collectives, exchange(): got = lax.all_to_all(flat, 'smp', split_axis=0, concat_axis=0, tiled=True)  27.1 us
    ppermute x10, starting transfers between devices, shifted(): return lax.ppermute(value, 'smp', pairs)  18.4 us
    all_to_all x1, starting transfers between devices, exchange(): got = lax.all_to_all(flat, 'smp', split_axis=0, concat_axis=0, tiled=True)  15.1 us
  transfers between devices with their start and end apart: 15, of which 9 were waited for; matrix products, arithmetic and copies ran while one was open for 0% of the time, Pallas kernels for 1%

profile of v3, /device:TPU:32, one launch (start us, length us, event | category | flops | bytes accessed | tf_op | source)
XLA Modules:
  0.0 105.9 jit_solution(14034385129202357095)
XLA Ops:
  0.6 0.1 collective-permute-start
  0.7 0.5 collective-permute-start.1
  1.2 1.5 %shard_map.122 = (s32[1,256]{1,0:T(1,128)S(1)}, f32[1,1024,256]{2,1,0:T(8,128)S(1)}, f32[10,1,256]{2,1,0:T(1,128)S(1)}, f32[10,1,128]{2,1,0:T(1,128)S(1)}, f32[1...) custom-call(s32[1,256]{1,0:T(1,128)} %bitcast.24, ...), custom_call_target="tpu_custom_call" | custom-call | tf_op jit(solution)/shard_map/pallas_call | solution.py:65
  2.7 0.0 collective-permute-done.1.mcf_peer
  2.7 0.0 collective-permute-done.cov_peer
  2.7 1.9 %shard_map.123 = (f32[2176,128]{1,0:T(8,128)}, f32[80,128]{1,0:T(8,128)S(1)}) custom-call(s32[1,256]{1,0:T(1,128)S(1)} %get-tuple-element.14.ids, f32[1,1024,256]{2,1,0:T(8,128)S(1)} %get-tuple-element.15.geno, f32[10,1,256]{2,1,0:T(1,128)S(1)} %get-tuple-element.16.cov, f32[10,1,256]{2,1,0:T(1,128)S(1)} %collective-permute-done.cov_peer, ...), custom_call_target="tpu_custom_call" | custom-call | tf_op jit(solution)/shard_map/pallas_call | solution.py:285
  4.7 15.1 %all-to-all-start = ((f32[128,1,2176]{2,1,0:T(1,128)}), f32[128,1,2176]{2,1,0:T(1,128)S(1)}, u32[]{:S(2)}, u32[]{:S(2)}) async-start(f32[128,1,2176]{2,1,0:T(1,128)} %bitcast.5), calls=%async_computation | async-start | bytes 2228224 | tf_op jit(solution)/shard_map/all_to_all | solution.py:257
  19.8 4.6 %collective-permute-start.2 = (f32[80,128]{1,0:T(8,128)S(1)}, f32[80,128]{1,0:T(8,128)S(1)}, u32[]{:S(2)}, u32[]{:S(2)}) collective-permute-start(f32[80,128]{1,0:T(8,128)S(1)} %get-tuple-element.23), channel_id=1, source_target_pairs={{0,16},{1,17},{2,18},{3,19},{4,20},{5,21},{6,22},{7,23},{8,24},{9,... | collective-permute-start | bytes 122888 | tf_op jit(solution)/shard_map/ppermute | solution.py:235
  24.4 25.3 %collective-permute-done.2 = f32[80,128]{1,0:T(8,128)S(1)} collective-permute-done((f32[80,128]{1,0:T(8,128)S(1)}, f32[80,128]{1,0:T(8,128)S(1)}, u32[]{:S(2)}, u32[]{:S(2)}) %collective-permute-start.2) | collective-permute-done | bytes 40992 | tf_op jit(solution)/shard_map/ppermute | solution.py:235
  49.7 0.5 collective-permute-start.4
  50.2 0.7 collective-permute-done.3
  50.9 0.1 collective-permute-done.4.mcs_peer
  51.0 1.5 %collective-permute-start.5 = (f32[80,128]{1,0:T(8,128)S(1)}, f32[80,128]{1,0:T(8,128)S(1)}, u32[]{:S(2)}, u32[]{:S(2)}) collective-permute-start(f32[80,128]{1,0:T(8,128)S(1)} %add.25), channel_id=1, source_target_pairs={{0,1},{1,2},{2,3},{3,0},{4,5},{5,6},{6,7},{7,4},{8,9},{9,10},{10,1... | collective-permute-start | bytes 122888 | tf_op jit(solution)/shard_map/ppermute | solution.py:235
  52.5 1.8 %collective-permute-start.6 = (f32[80,128]{1,0:T(8,128)S(1)}, f32[80,128]{1,0:T(8,128)S(1)}, u32[]{:S(2)}, u32[]{:S(2)}) collective-permute-start(f32[80,128]{1,0:T(8,128)S(1)} %add.25), channel_id=1, source_target_pairs={{0,3},{1,0},{2,1},{3,2},{4,7},{5,4},{6,5},{7,6},{8,11},{9,8},{10,9... | collective-permute-start | bytes 122888 | tf_op jit(solution)/shard_map/ppermute | solution.py:235
  54.3 1.8 %collective-permute-start.7 = (f32[80,128]{1,0:T(8,128)S(1)}, f32[80,128]{1,0:T(8,128)S(1)}, u32[]{:S(2)}, u32[]{:S(2)}) collective-permute-start(f32[80,128]{1,0:T(8,128)S(1)} %add.25), channel_id=1, source_target_pairs={{0,2},{1,3},{2,0},{3,1},{4,6},{5,7},{6,4},{7,5},{8,10},{9,11},{10,... | collective-permute-start | bytes 122888 | tf_op jit(solution)/shard_map/ppermute | solution.py:235
  56.0 0.2 collective-permute-done.5
  56.2 0.3 collective-permute-done.6
  56.5 3.3 %collective-permute-done.7 = f32[80,128]{1,0:T(8,128)S(1)} collective-permute-done((f32[80,128]{1,0:T(8,128)S(1)}, f32[80,128]{1,0:T(8,128)S(1)}, u32[]{:S(2)}, u32[]{:S(2)}) %collective-permute-start.7) | collective-permute-done | bytes 40992 | tf_op jit(solution)/shard_map/ppermute | solution.py:235
  59.8 3.5 %collective-permute-start.10 = (f32[80,128]{1,0:T(8,128)S(1)}, f32[80,128]{1,0:T(8,128)S(1)}, u32[]{:S(2)}, u32[]{:S(2)}) collective-permute-start(f32[80,128]{1,0:T(8,128)S(1)} %add_add_fusion.1), channel_id=1, source_target_pairs={{0,64},{1,65},{2,66},{3,67},{4,68},{5,69},{6,70},{7,71},{8,72},{9,... | collective-permute-start | bytes 122888 | tf_op jit(solution)/shard_map/ppermute | solution.py:235
  63.3 0.8 collective-permute-start.8
  64.1 2.5 %collective-permute-start.9 = (f32[80,128]{1,0:T(8,128)S(1)}, f32[80,128]{1,0:T(8,128)S(1)}, u32[]{:S(2)}, u32[]{:S(2)}) collective-permute-start(f32[80,128]{1,0:T(8,128)S(1)} %add_add_fusion.1), channel_id=1, source_target_pairs={{0,96},{1,97},{2,98},{3,99},{4,100},{5,101},{6,102},{7,103},{8,104... | collective-permute-start | bytes 122888 | tf_op jit(solution)/shard_map/ppermute | solution.py:235
  66.5 0.0 collective-permute-done.10
  66.5 2.0 %collective-permute-done.8 = f32[80,128]{1,0:T(8,128)S(1)} collective-permute-done((f32[80,128]{1,0:T(8,128)S(1)}, f32[80,128]{1,0:T(8,128)S(1)}, u32[]{:S(2)}, u32[]{:S(2)}) %collective-permute-start.8) | collective-permute-done | bytes 40992 | tf_op jit(solution)/shard_map/ppermute | solution.py:235
  68.5 0.1 collective-permute-start.11
  68.7 2.0 %collective-permute-start.12 = (f32[80,128]{1,0:T(8,128)S(1)}, f32[80,128]{1,0:T(8,128)S(1)}, u32[]{:S(2)}, u32[]{:S(2)}) collective-permute-start(f32[80,128]{1,0:T(8,128)S(1)} %add_add_fusion.w_0), channel_id=1, source_target_pairs={{0,28},{1,29},{2,30},{3,31},{4,0},{5,1},{6,2},{7,3},{8,4},{9,5},{1... | collective-permute-start | bytes 122888 | tf_op jit(solution)/shard_map/ppermute | solution.py:235
  70.6 0.0 collective-permute-start.13
  70.6 2.3 %collective-permute-done.11.w_1 = f32[80,128]{1,0:T(8,128)S(1)} collective-permute-done((f32[80,128]{1,0:T(8,128)S(1)}, f32[80,128]{1,0:T(8,128)S(1)}, u32[]{:S(2)}, u32[]{:S(2)}) %collective-permute-start.11) | collective-permute-done | bytes 40992 | tf_op jit(solution)/shard_map/ppermute | solution.py:235
  72.9 3.8 %collective-permute-done.13.w_3 = f32[80,128]{1,0:T(8,128)S(1)} collective-permute-done((f32[80,128]{1,0:T(8,128)S(1)}, f32[80,128]{1,0:T(8,128)S(1)}, u32[]{:S(2)}, u32[]{:S(2)}) %collective-permute-start.13) | collective-permute-done | bytes 40992 | tf_op jit(solution)/shard_map/ppermute | solution.py:235
  76.7 0.0 all-to-all-done
  76.8 1.2 %shard_map.124 = f32[1280,128]{1,0:T(8,128)S(1)} custom-call(f32[2176,128]{1,0:T(8,128)S(1)} %bitcast.11, f32[80,128]{1,0:T(8,128)S(1)} %add_add_fusion.w_0, f32[80,128]{1,0:T(8,128)S(1)} %collective-permute-done.11.w_1, f32[80,128]{1,0:T(8,128)S(1)} %collective-permute-done.12.w_2, f32[80,128]{1,0:T(8,128)S(1)} %collective-permute-done.13.w_3, ...), custom_call_target="tpu_custom_call" | custom-call | tf_op jit(solution)/shard_map/pallas_call | solution.py:304
  78.0 27.1 %all_to_all.10 = f32[128,1,1280]{2,1,0:T(1,128)S(1)} all-to-all(f32[128,1,1280]{2,1,0:T(1,128)S(1)} %bitcast.13), channel_id=1, replica_groups=mesh['srv'=2,'smp'=128] {'smp'}, dimensions={0} | all-to-all | bytes 1310720 | tf_op jit(solution)/shard_map/all_to_all | solution.py:257
  105.0 0.8 shard_map.125
  (15 shorter events, 0.1 us)
Async XLA Ops:
  0.6 2.1 %collective-permute-start = (f32[10,1,256]{2,1,0:T(1,128)}, f32[10,1,256]{2,1,0:T(1,128)S(1)}, u32[]{:S(2)}, u32[]{:S(2)}) collective-permute-start(f32[10,1,256]{2,1,0:T(1,128)} %bitcast.20), channel_id=1, source_target_pairs={{0,128},{128,0},{1,129},{129,1},{2,130},{130,2},{3,131},{131,3},{4... | collective-permute-start | bytes 30728 | tf_op jit(solution)/shard_map/ppermute | solution.py:221
  0.7 2.0 %collective-permute-start.1 = (f32[10,1,128]{2,1,0:T(1,128)}, f32[10,1,128]{2,1,0:T(1,128)S(1)}, u32[]{:S(2)}, u32[]{:S(2)}) collective-permute-start(f32[10,1,128]{2,1,0:T(1,128)} %bitcast.22), channel_id=1, source_target_pairs={{0,128},{128,0},{1,129},{129,1},{2,130},{130,2},{3,131},{131,3},{4... | collective-permute-start | bytes 15368 | tf_op jit(solution)/shard_map/ppermute | solution.py:221
  4.7 45.0 %copy-start.3 = (f32[1,10,128]{2,0,1:T(1,128)S(1)}, f32[1,10,128]{2,0,1:T(1,128)}, u32[]{:S(2)}) copy-start(f32[1,10,128]{2,0,1:T(1,128)} %param.17) | copy-start | bytes 15364
  4.7 72.1 %copy-start = (f32[1,1024,128]{2,1,0:T(8,128)S(1)}, f32[1,1024,128]{2,1,0:T(8,128)}, u32[]{:S(2)}) copy-start(f32[1,1024,128]{2,1,0:T(8,128)} %prod_second.1) | copy-start | bytes 1572868
  4.7 72.1 %copy-start.1 = (f32[1,10,1024]{2,0,1:T(1,128)S(1)}, f32[1,10,1024]{2,0,1:T(1,128)}, u32[]{:S(2)}) copy-start(f32[1,10,1024]{2,0,1:T(1,128)} %param.18) | copy-start | bytes 122884
  4.7 72.1 %copy-start.2 = (f32[128,32]{0,1:T(8,128)S(1)}, f32[128,32]{0,1:T(8,128)}, u32[]{:S(2)}) copy-start(f32[128,32]{0,1:T(8,128)} %param.21) | copy-start | bytes 49156
  4.7 72.1 %all-to-all-start = ((f32[128,1,2176]{2,1,0:T(1,128)}), f32[128,1,2176]{2,1,0:T(1,128)S(1)}, u32[]{:S(2)}, u32[]{:S(2)}) async-start(f32[128,1,2176]{2,1,0:T(1,128)} %bitcast.5), calls=%async_computation | async-start | bytes 2228224 | tf_op jit(solution)/shard_map/all_to_all | solution.py:257
  19.8 29.9 %collective-permute-start.2 = (f32[80,128]{1,0:T(8,128)S(1)}, f32[80,128]{1,0:T(8,128)S(1)}, u32[]{:S(2)}, u32[]{:S(2)}) collective-permute-start(f32[80,128]{1,0:T(8,128)S(1)} %get-tuple-element.23), channel_id=1, source_target_pairs={{0,16},{1,17},{2,18},{3,19},{4,20},{5,21},{6,22},{7,23},{8,24},{9,... | collective-permute-start | bytes 122888 | tf_op jit(solution)/shard_map/ppermute | solution.py:235
  49.7 1.2 %collective-permute-start.3 = (f32[80,128]{1,0:T(8,128)S(1)}, f32[80,128]{1,0:T(8,128)S(1)}, u32[]{:S(2)}, u32[]{:S(2)}) collective-permute-start(f32[80,128]{1,0:T(8,128)S(1)} %add.24), channel_id=1, source_target_pairs={{0,128},{128,0},{1,129},{129,1},{2,130},{130,2},{3,131},{131,3},{4... | collective-permute-start | bytes 122888 | tf_op jit(solution)/shard_map/ppermute | solution.py:221
  49.7 1.3 %collective-permute-start.4 = (f32[10,1,128]{2,1,0:T(1,128)S(1)}, f32[10,1,128]{2,1,0:T(1,128)S(1)}, u32[]{:S(2)}, u32[]{:S(2)}) collective-permute-start(f32[10,1,128]{2,1,0:T(1,128)S(1)} %bitcast.17), channel_id=1, source_target_pairs={{0,128},{128,0},{1,129},{129,1},{2,130},{130,2},{3,131},{131,3},{4... | collective-permute-start | bytes 15368 | tf_op jit(solution)/shard_map/ppermute | solution.py:221
  51.0 5.2 %collective-permute-start.5 = (f32[80,128]{1,0:T(8,128)S(1)}, f32[80,128]{1,0:T(8,128)S(1)}, u32[]{:S(2)}, u32[]{:S(2)}) collective-permute-start(f32[80,128]{1,0:T(8,128)S(1)} %add.25), channel_id=1, source_target_pairs={{0,1},{1,2},{2,3},{3,0},{4,5},{5,6},{6,7},{7,4},{8,9},{9,10},{10,1... | collective-permute-start | bytes 122888 | tf_op jit(solution)/shard_map/ppermute | solution.py:235
  52.5 4.0 %collective-permute-start.6 = (f32[80,128]{1,0:T(8,128)S(1)}, f32[80,128]{1,0:T(8,128)S(1)}, u32[]{:S(2)}, u32[]{:S(2)}) collective-permute-start(f32[80,128]{1,0:T(8,128)S(1)} %add.25), channel_id=1, source_target_pairs={{0,3},{1,0},{2,1},{3,2},{4,7},{5,4},{6,5},{7,6},{8,11},{9,8},{10,9... | collective-permute-start | bytes 122888 | tf_op jit(solution)/shard_map/ppermute | solution.py:235
  54.3 5.5 %collective-permute-start.7 = (f32[80,128]{1,0:T(8,128)S(1)}, f32[80,128]{1,0:T(8,128)S(1)}, u32[]{:S(2)}, u32[]{:S(2)}) collective-permute-start(f32[80,128]{1,0:T(8,128)S(1)} %add.25), channel_id=1, source_target_pairs={{0,2},{1,3},{2,0},{3,1},{4,6},{5,7},{6,4},{7,5},{8,10},{9,11},{10,... | collective-permute-start | bytes 122888 | tf_op jit(solution)/shard_map/ppermute | solution.py:235
  59.8 6.7 %collective-permute-start.10 = (f32[80,128]{1,0:T(8,128)S(1)}, f32[80,128]{1,0:T(8,128)S(1)}, u32[]{:S(2)}, u32[]{:S(2)}) collective-permute-start(f32[80,128]{1,0:T(8,128)S(1)} %add_add_fusion.1), channel_id=1, source_target_pairs={{0,64},{1,65},{2,66},{3,67},{4,68},{5,69},{6,70},{7,71},{8,72},{9,... | collective-permute-start | bytes 122888 | tf_op jit(solution)/shard_map/ppermute | solution.py:235
  63.3 5.2 %collective-permute-start.8 = (f32[80,128]{1,0:T(8,128)S(1)}, f32[80,128]{1,0:T(8,128)S(1)}, u32[]{:S(2)}, u32[]{:S(2)}) collective-permute-start(f32[80,128]{1,0:T(8,128)S(1)} %add_add_fusion.1), channel_id=1, source_target_pairs={{0,32},{1,33},{2,34},{3,35},{4,36},{5,37},{6,38},{7,39},{8,40},{9,... | collective-permute-start | bytes 122888 | tf_op jit(solution)/shard_map/ppermute | solution.py:235
  64.1 4.4 %collective-permute-start.9 = (f32[80,128]{1,0:T(8,128)S(1)}, f32[80,128]{1,0:T(8,128)S(1)}, u32[]{:S(2)}, u32[]{:S(2)}) collective-permute-start(f32[80,128]{1,0:T(8,128)S(1)} %add_add_fusion.1), channel_id=1, source_target_pairs={{0,96},{1,97},{2,98},{3,99},{4,100},{5,101},{6,102},{7,103},{8,104... | collective-permute-start | bytes 122888 | tf_op jit(solution)/shard_map/ppermute | solution.py:235
  68.5 4.4 %collective-permute-start.11 = (f32[80,128]{1,0:T(8,128)S(1)}, f32[80,128]{1,0:T(8,128)S(1)}, u32[]{:S(2)}, u32[]{:S(2)}) collective-permute-start(f32[80,128]{1,0:T(8,128)S(1)} %add_add_fusion.w_0), channel_id=1, source_target_pairs={{0,4},{1,5},{2,6},{3,7},{4,8},{5,9},{6,10},{7,11},{8,12},{9,13},{1... | collective-permute-start | bytes 122888 | tf_op jit(solution)/shard_map/ppermute | solution.py:235
  68.7 4.2 %collective-permute-start.12 = (f32[80,128]{1,0:T(8,128)S(1)}, f32[80,128]{1,0:T(8,128)S(1)}, u32[]{:S(2)}, u32[]{:S(2)}) collective-permute-start(f32[80,128]{1,0:T(8,128)S(1)} %add_add_fusion.w_0), channel_id=1, source_target_pairs={{0,28},{1,29},{2,30},{3,31},{4,0},{5,1},{6,2},{7,3},{8,4},{9,5},{1... | collective-permute-start | bytes 122888 | tf_op jit(solution)/shard_map/ppermute | solution.py:235
  70.6 6.1 %collective-permute-start.13 = (f32[80,128]{1,0:T(8,128)S(1)}, f32[80,128]{1,0:T(8,128)S(1)}, u32[]{:S(2)}, u32[]{:S(2)}) collective-permute-start(f32[80,128]{1,0:T(8,128)S(1)} %add_add_fusion.w_0), channel_id=1, source_target_pairs={{0,8},{1,9},{2,10},{3,11},{4,12},{5,13},{6,14},{7,15},{8,16},{9,17... | collective-permute-start | bytes 122888 | tf_op jit(solution)/shard_map/ppermute | solution.py:235

commit v4 on v3

--- a/solution.py
+++ b/solution.py
@@ -120,6 +120,11 @@
             for k in range(K):
                 out = out + table[:, k : k + 1] * gram[k : k + 1, :]
             weight[pl.ds(c * K, K), :] = out
+    near = lax.axis_index("srv") == 0
+    reach = weight.shape[0] // 2
+    low, high = weight[0:reach, :], weight[reach:, :]
+    weight[0:reach, :] = jnp.where(near, low, high)
+    weight[reach:, :] = jnp.where(near, high, low)
     side = jnp.concatenate(
         [cov_sum, spot.astype(jnp.float32), jnp.zeros((64 - K - 1, width), jnp.float32)], axis=0
     )
@@ -132,7 +137,7 @@
     payload[pl.ds(2 * chunks, LANES, stride=rows), :] = extra
 
 
-def fit_kernel(recv, w_0, w_1, w_2, w_3, mw, mcs, mcs_peer, prod_second, phen, payload, a_s, b_s):
+def fit_kernel(recv, mine, theirs, mw, mcs, mcs_peer, prod_second, phen, payload, a_s, b_s):
     variants = prod_second.shape[1]
     chunks = variants // LANES
     rows = 2 * chunks + 1
@@ -155,10 +160,14 @@
     b_s[0:K, :] = open_second
     b_s[16 : 16 + K, :] = own_mask + leader * open_second
     a_s[...] = jnp.zeros_like(a_s)
-    ow = w_0[...] + w_1[...] + w_2[...] + w_3[...]
+    near = lax.axis_index("srv") == 0
+    ow = (jnp.where(near, mine[...], theirs[...]), jnp.where(near, theirs[...], mine[...]))
+    reach = chunks // 2
     for c in range(chunks):
         a_s[0:K, pl.ds(c * LANES, LANES)] = chunk_of(mw, c)
-        a_s[16 : 16 + K, pl.ds(c * LANES, LANES)] = ow[c * K : (c + 1) * K]
+        a_s[16 : 16 + K, pl.ds(c * LANES, LANES)] = ow[c // reach][
+            c % reach * K : (c % reach + 1) * K
+        ]
     spots = jnp.concatenate(place, axis=0)
     a_high, a_mid, a_low = parts(a_s[...])
     b_high, b_mid, b_low = parts(b_s[...])
@@ -295,16 +304,18 @@
     received = exchange(packed, peers)
     other = z_opposite(weight)
     weight = weight + other
-    weight = weight + swap(weight)
+    reach = weight.shape[0] // 2
+    weight = weight[:reach] + swap(weight[reach:])
     mcs_peer = swap(mcs)
     weight, mcs_peer = lax.optimization_barrier((weight, mcs_peer))
     weight = total(terms(weight, (0, 0, 1), (0, 0, 3), (0, 0, 2)))
     weight = total(terms(weight, (1, 0, 0), (3, 0, 0), (2, 0, 0)))
-    open_weight = terms(weight, (0, 1, 0), (0, 7, 0), (0, 2, 0))
+    weight = total(terms(weight, (0, 1, 0), (0, 7, 0), (0, 2, 0)))
+    open_weight = (weight, swap(weight))
     fitted = pl.pallas_call(
         fit_kernel,
         out_shape=jax.ShapeDtypeStruct((variants // 8 * 10, LANES), jnp.float32),
-        in_specs=[VMEM] * 10,
+        in_specs=[VMEM] * 8,
         out_specs=VMEM,
         compiler_params=ROOM,
         scratch_shapes=[

time: 106 us -> 112 us (1.057)
  blocking collectives: 27.1 us -> 31.8 us
    all_to_all x1, blocking collectives: 27.1 us -> 31.8 us  [exchange(): got = lax.all_to_all(flat, 'smp', split_axis=0, concat_axis=0, tiled=True)]
    ppermute x4 -> x5, waiting for transfers between devices: 0.82 us -> 2 us  [swap(): return lax.ppermute(value, 'srv', [(0, 1), (1, 0)])]
  transfers between devices with their start and end apart: 15 -> 16, of which waited for: 9 -> 10; matrix products, arithmetic and copies ran while one was open for 0% -> 0% of each run, Pallas kernels for 1% -> 1%
where the time goes in v4:
time: 112 us; the launch traced here: 111 us
  waiting for transfers between devices  38.4 us (34%)
  starting transfers between devices  35 us (31%)
  blocking collectives  31.8 us (28%)
  Pallas kernels  5.48 us (5%)
    ppermute x10, waiting for transfers between devices, shifted(): return lax.ppermute(value, 'smp', pairs)  36.4 us
    all_to_all x1, blocking collectives, exchange(): got = lax.all_to_all(flat, 'smp', split_axis=0, concat_axis=0, tiled=True)  31.8 us
    ppermute x10, starting transfers between devices, shifted(): return lax.ppermute(value, 'smp', pairs)  18.4 us
    all_to_all x1, starting transfers between devices, exchange(): got = lax.all_to_all(flat, 'smp', split_axis=0, concat_axis=0, tiled=True)  15.1 us
  transfers between devices with their start and end apart: 16, of which 10 were waited for; matrix products, arithmetic and copies ran while one was open for 0% of the time, Pallas kernels for 1%

profile of v4, /device:TPU:32, one launch (start us, length us, event | category | flops | bytes accessed | tf_op | source)
XLA Modules:
  0.0 111.5 jit_solution(2119406703589117736)
XLA Ops:
  0.6 0.1 collective-permute-start
  0.7 0.5 collective-permute-start.1
  1.2 1.5 %shard_map.122 = (s32[1,256]{1,0:T(1,128)S(1)}, f32[1,1024,256]{2,1,0:T(8,128)S(1)}, f32[10,1,256]{2,1,0:T(1,128)S(1)}, f32[10,1,128]{2,1,0:T(1,128)S(1)}, f32[1...) custom-call(s32[1,256]{1,0:T(1,128)} %bitcast.24, ...), custom_call_target="tpu_custom_call" | custom-call | tf_op jit(solution)/shard_map/pallas_call | solution.py:65
  2.7 0.0 collective-permute-done.1.mcf_peer
  2.7 0.0 collective-permute-done.cov_peer
  2.7 2.0 %shard_map.123 = (f32[2176,128]{1,0:T(8,128)}, f32[80,128]{1,0:T(8,128)S(1)}) custom-call(s32[1,256]{1,0:T(1,128)S(1)} %get-tuple-element.14.ids, f32[1,1024,256]{2,1,0:T(8,128)S(1)} %get-tuple-element.15.geno, f32[10,1,256]{2,1,0:T(1,128)S(1)} %get-tuple-element.16.cov, f32[10,1,256]{2,1,0:T(1,128)S(1)} %collective-permute-done.cov_peer, ...), custom_call_target="tpu_custom_call" | custom-call | tf_op jit(solution)/shard_map/pallas_call | solution.py:294
  4.7 15.1 %all-to-all-start = ((f32[128,1,2176]{2,1,0:T(1,128)}), f32[128,1,2176]{2,1,0:T(1,128)S(1)}, u32[]{:S(2)}, u32[]{:S(2)}) async-start(f32[128,1,2176]{2,1,0:T(1,128)} %bitcast.5), calls=%async_computation | async-start | bytes 2228224 | tf_op jit(solution)/shard_map/all_to_all | solution.py:266
  19.8 4.6 %collective-permute-start.2 = (f32[80,128]{1,0:T(8,128)S(1)}, f32[80,128]{1,0:T(8,128)S(1)}, u32[]{:S(2)}, u32[]{:S(2)}) collective-permute-start(f32[80,128]{1,0:T(8,128)S(1)} %get-tuple-element.23), channel_id=1, source_target_pairs={{0,16},{1,17},{2,18},{3,19},{4,20},{5,21},{6,22},{7,23},{8,24},{9,... | collective-permute-start | bytes 122888 | tf_op jit(solution)/shard_map/ppermute | solution.py:244
  24.4 25.3 %collective-permute-done.2 = f32[80,128]{1,0:T(8,128)S(1)} collective-permute-done((f32[80,128]{1,0:T(8,128)S(1)}, f32[80,128]{1,0:T(8,128)S(1)}, u32[]{:S(2)}, u32[]{:S(2)}) %collective-permute-start.2) | collective-permute-done | bytes 40992 | tf_op jit(solution)/shard_map/ppermute | solution.py:244
  49.7 0.1 collective-permute-start.3
  49.8 0.5 collective-permute-start.4
  50.3 0.7 collective-permute-done.3
  51.0 0.1 collective-permute-done.4.mcs_peer
  51.1 1.5 %collective-permute-start.5 = (f32[40,128]{1,0:T(8,128)S(1)}, f32[40,128]{1,0:T(8,128)S(1)}, u32[]{:S(2)}, u32[]{:S(2)}) collective-permute-start(f32[40,128]{1,0:T(8,128)S(1)} %slice_add_fusion), channel_id=1, source_target_pairs={{0,1},{1,2},{2,3},{3,0},{4,5},{5,6},{6,7},{7,4},{8,9},{9,10},{10,1... | collective-permute-start | bytes 61448 | tf_op jit(solution)/shard_map/ppermute | solution.py:244
  52.6 1.8 %collective-permute-start.6 = (f32[40,128]{1,0:T(8,128)S(1)}, f32[40,128]{1,0:T(8,128)S(1)}, u32[]{:S(2)}, u32[]{:S(2)}) collective-permute-start(f32[40,128]{1,0:T(8,128)S(1)} %slice_add_fusion), channel_id=1, source_target_pairs={{0,3},{1,0},{2,1},{3,2},{4,7},{5,4},{6,5},{7,6},{8,11},{9,8},{10,9... | collective-permute-start | bytes 61448 | tf_op jit(solution)/shard_map/ppermute | solution.py:244
  54.4 1.8 %collective-permute-start.7 = (f32[40,128]{1,0:T(8,128)S(1)}, f32[40,128]{1,0:T(8,128)S(1)}, u32[]{:S(2)}, u32[]{:S(2)}) collective-permute-start(f32[40,128]{1,0:T(8,128)S(1)} %slice_add_fusion), channel_id=1, source_target_pairs={{0,2},{1,3},{2,0},{3,1},{4,6},{5,7},{6,4},{7,5},{8,10},{9,11},{10,... | collective-permute-start | bytes 61448 | tf_op jit(solution)/shard_map/ppermute | solution.py:244
  56.1 0.2 collective-permute-done.6
  56.4 3.3 %collective-permute-done.7 = f32[40,128]{1,0:T(8,128)S(1)} collective-permute-done((f32[40,128]{1,0:T(8,128)S(1)}, f32[40,128]{1,0:T(8,128)S(1)}, u32[]{:S(2)}, u32[]{:S(2)}) %collective-permute-start.7) | collective-permute-done | bytes 20512 | tf_op jit(solution)/shard_map/ppermute | solution.py:244
  59.7 3.5 %collective-permute-start.10 = (f32[40,128]{1,0:T(8,128)S(1)}, f32[40,128]{1,0:T(8,128)S(1)}, u32[]{:S(2)}, u32[]{:S(2)}) collective-permute-start(f32[40,128]{1,0:T(8,128)S(1)} %add_add_fusion.2), channel_id=1, source_target_pairs={{0,64},{1,65},{2,66},{3,67},{4,68},{5,69},{6,70},{7,71},{8,72},{9,... | collective-permute-start | bytes 61448 | tf_op jit(solution)/shard_map/ppermute | solution.py:244
  63.2 0.8 collective-permute-start.8
  63.9 2.5 %collective-permute-start.9 = (f32[40,128]{1,0:T(8,128)S(1)}, f32[40,128]{1,0:T(8,128)S(1)}, u32[]{:S(2)}, u32[]{:S(2)}) collective-permute-start(f32[40,128]{1,0:T(8,128)S(1)} %add_add_fusion.2), channel_id=1, source_target_pairs={{0,96},{1,97},{2,98},{3,99},{4,100},{5,101},{6,102},{7,103},{8,104... | collective-permute-start | bytes 61448 | tf_op jit(solution)/shard_map/ppermute | solution.py:244
  66.4 1.8 %collective-permute-done.8 = f32[40,128]{1,0:T(8,128)S(1)} collective-permute-done((f32[40,128]{1,0:T(8,128)S(1)}, f32[40,128]{1,0:T(8,128)S(1)}, u32[]{:S(2)}, u32[]{:S(2)}) %collective-permute-start.8) | collective-permute-done | bytes 20512 | tf_op jit(solution)/shard_map/ppermute | solution.py:244
  68.2 0.1 collective-permute-start.11
  68.3 2.0 %collective-permute-start.12 = (f32[40,128]{1,0:T(8,128)S(1)}, f32[40,128]{1,0:T(8,128)S(1)}, u32[]{:S(2)}, u32[]{:S(2)}) collective-permute-start(f32[40,128]{1,0:T(8,128)S(1)} %add_add_fusion.1), channel_id=1, source_target_pairs={{0,28},{1,29},{2,30},{3,31},{4,0},{5,1},{6,2},{7,3},{8,4},{9,5},{1... | collective-permute-start | bytes 61448 | tf_op jit(solution)/shard_map/ppermute | solution.py:244
  70.3 1.8 %collective-permute-done.11 = f32[40,128]{1,0:T(8,128)S(1)} collective-permute-done((f32[40,128]{1,0:T(8,128)S(1)}, f32[40,128]{1,0:T(8,128)S(1)}, u32[]{:S(2)}, u32[]{:S(2)}) %collective-permute-start.11) | collective-permute-done | bytes 20512 | tf_op jit(solution)/shard_map/ppermute | solution.py:244
  72.1 0.1 collective-permute-done.12
  72.1 4.0 %collective-permute-done.13 = f32[40,128]{1,0:T(8,128)S(1)} collective-permute-done((f32[40,128]{1,0:T(8,128)S(1)}, f32[40,128]{1,0:T(8,128)S(1)}, u32[]{:S(2)}, u32[]{:S(2)}) %collective-permute-start.13) | collective-permute-done | bytes 20512 | tf_op jit(solution)/shard_map/ppermute | solution.py:244
  76.2 0.3 collective-permute-start.14
  76.5 1.2 %collective-permute-done.14.theirs = f32[40,128]{1,0:T(8,128)S(1)} collective-permute-done((f32[40,128]{1,0:T(8,128)S(1)}, f32[40,128]{1,0:T(8,128)S(1)}, u32[]{:S(2)}, u32[]{:S(2)}) %collective-permute-start.14) | collective-permute-done | bytes 20512 | tf_op jit(solution)/shard_map/ppermute | solution.py:230
  77.7 1.2 %shard_map.124 = f32[1280,128]{1,0:T(8,128)S(1)} custom-call(f32[2176,128]{1,0:T(8,128)S(1)} %bitcast.11, f32[40,128]{1,0:T(8,128)S(1)} %add_add_fusion.mine, f32[40,128]{1,0:T(8,128)S(1)} %collective-permute-done.14.theirs, f32[80,128]{1,0:T(8,128)S(1)} %bitcast.15, f32[10,1,128]{2,1,0:T(1,128)S(1)} %bitcast.18, ...), custom_call_target="tpu_custom_call" | custom-call | tf_op jit(solution)/shard_map/pallas_call | solution.py:315
  78.9 31.8 %all_to_all.10 = f32[128,1,1280]{2,1,0:T(1,128)S(1)} all-to-all(f32[128,1,1280]{2,1,0:T(1,128)S(1)} %bitcast.13), channel_id=1, replica_groups=mesh['srv'=2,'smp'=128] {'smp'}, dimensions={0} | all-to-all | bytes 1310720 | tf_op jit(solution)/shard_map/all_to_all | solution.py:266
  110.6 0.8 shard_map.125
  (19 shorter events, 0.1 us)
Async XLA Ops:
  0.6 2.1 %collective-permute-start = (f32[10,1,256]{2,1,0:T(1,128)}, f32[10,1,256]{2,1,0:T(1,128)S(1)}, u32[]{:S(2)}, u32[]{:S(2)}) collective-permute-start(f32[10,1,256]{2,1,0:T(1,128)} %bitcast.20), channel_id=1, source_target_pairs={{0,128},{128,0},{1,129},{129,1},{2,130},{130,2},{3,131},{131,3},{4... | collective-permute-start | bytes 30728 | tf_op jit(solution)/shard_map/ppermute | solution.py:230
  0.7 2.0 %collective-permute-start.1 = (f32[10,1,128]{2,1,0:T(1,128)}, f32[10,1,128]{2,1,0:T(1,128)S(1)}, u32[]{:S(2)}, u32[]{:S(2)}) collective-permute-start(f32[10,1,128]{2,1,0:T(1,128)} %bitcast.22), channel_id=1, source_target_pairs={{0,128},{128,0},{1,129},{129,1},{2,130},{130,2},{3,131},{131,3},{4... | collective-permute-start | bytes 15368 | tf_op jit(solution)/shard_map/ppermute | solution.py:230
  4.7 45.1 %copy-start.3 = (f32[1,10,128]{2,0,1:T(1,128)S(1)}, f32[1,10,128]{2,0,1:T(1,128)}, u32[]{:S(2)}) copy-start(f32[1,10,128]{2,0,1:T(1,128)} %param.17) | copy-start | bytes 15364
  4.7 72.9 %copy-start = (f32[1,1024,128]{2,1,0:T(8,128)S(1)}, f32[1,1024,128]{2,1,0:T(8,128)}, u32[]{:S(2)}) copy-start(f32[1,1024,128]{2,1,0:T(8,128)} %prod_second.1) | copy-start | bytes 1572868
  4.7 72.9 %copy-start.1 = (f32[1,10,1024]{2,0,1:T(1,128)S(1)}, f32[1,10,1024]{2,0,1:T(1,128)}, u32[]{:S(2)}) copy-start(f32[1,10,1024]{2,0,1:T(1,128)} %param.18) | copy-start | bytes 122884
  4.7 72.9 %copy-start.2 = (f32[128,32]{0,1:T(8,128)S(1)}, f32[128,32]{0,1:T(8,128)}, u32[]{:S(2)}) copy-start(f32[128,32]{0,1:T(8,128)} %param.21) | copy-start | bytes 49156
  4.7 72.9 %all-to-all-start = ((f32[128,1,2176]{2,1,0:T(1,128)}), f32[128,1,2176]{2,1,0:T(1,128)S(1)}, u32[]{:S(2)}, u32[]{:S(2)}) async-start(f32[128,1,2176]{2,1,0:T(1,128)} %bitcast.5), calls=%async_computation | async-start | bytes 2228224 | tf_op jit(solution)/shard_map/all_to_all | solution.py:266
  19.8 29.8 %collective-permute-start.2 = (f32[80,128]{1,0:T(8,128)S(1)}, f32[80,128]{1,0:T(8,128)S(1)}, u32[]{:S(2)}, u32[]{:S(2)}) collective-permute-start(f32[80,128]{1,0:T(8,128)S(1)} %get-tuple-element.23), channel_id=1, source_target_pairs={{0,16},{1,17},{2,18},{3,19},{4,20},{5,21},{6,22},{7,23},{8,24},{9,... | collective-permute-start | bytes 122888 | tf_op jit(solution)/shard_map/ppermute | solution.py:244
  49.7 1.3 %collective-permute-start.3 = (f32[40,128]{1,0:T(8,128)S(1)}, f32[40,128]{1,0:T(8,128)S(1)}, u32[]{:S(2)}, u32[]{:S(2)}) collective-permute-start(f32[40,128]{1,0:T(8,128)S(1)} %slice.9), channel_id=1, source_target_pairs={{0,128},{128,0},{1,129},{129,1},{2,130},{130,2},{3,131},{131,3},{4... | collective-permute-start | bytes 61448 | tf_op jit(solution)/shard_map/ppermute | solution.py:230
  49.8 1.3 %collective-permute-start.4 = (f32[10,1,128]{2,1,0:T(1,128)S(1)}, f32[10,1,128]{2,1,0:T(1,128)S(1)}, u32[]{:S(2)}, u32[]{:S(2)}) collective-permute-start(f32[10,1,128]{2,1,0:T(1,128)S(1)} %bitcast.17), channel_id=1, source_target_pairs={{0,128},{128,0},{1,129},{129,1},{2,130},{130,2},{3,131},{131,3},{4... | collective-permute-start | bytes 15368 | tf_op jit(solution)/shard_map/ppermute | solution.py:230
  51.1 5.0 %collective-permute-start.5 = (f32[40,128]{1,0:T(8,128)S(1)}, f32[40,128]{1,0:T(8,128)S(1)}, u32[]{:S(2)}, u32[]{:S(2)}) collective-permute-start(f32[40,128]{1,0:T(8,128)S(1)} %slice_add_fusion), channel_id=1, source_target_pairs={{0,1},{1,2},{2,3},{3,0},{4,5},{5,6},{6,7},{7,4},{8,9},{9,10},{10,1... | collective-permute-start | bytes 61448 | tf_op jit(solution)/shard_map/ppermute | solution.py:244
  52.6 3.8 %collective-permute-start.6 = (f32[40,128]{1,0:T(8,128)S(1)}, f32[40,128]{1,0:T(8,128)S(1)}, u32[]{:S(2)}, u32[]{:S(2)}) collective-permute-start(f32[40,128]{1,0:T(8,128)S(1)} %slice_add_fusion), channel_id=1, source_target_pairs={{0,3},{1,0},{2,1},{3,2},{4,7},{5,4},{6,5},{7,6},{8,11},{9,8},{10,9... | collective-permute-start | bytes 61448 | tf_op jit(solution)/shard_map/ppermute | solution.py:244
  54.4 5.3 %collective-permute-start.7 = (f32[40,128]{1,0:T(8,128)S(1)}, f32[40,128]{1,0:T(8,128)S(1)}, u32[]{:S(2)}, u32[]{:S(2)}) collective-permute-start(f32[40,128]{1,0:T(8,128)S(1)} %slice_add_fusion), channel_id=1, source_target_pairs={{0,2},{1,3},{2,0},{3,1},{4,6},{5,7},{6,4},{7,5},{8,10},{9,11},{10,... | collective-permute-start | bytes 61448 | tf_op jit(solution)/shard_map/ppermute | solution.py:244
  59.7 6.7 %collective-permute-start.10 = (f32[40,128]{1,0:T(8,128)S(1)}, f32[40,128]{1,0:T(8,128)S(1)}, u32[]{:S(2)}, u32[]{:S(2)}) collective-permute-start(f32[40,128]{1,0:T(8,128)S(1)} %add_add_fusion.2), channel_id=1, source_target_pairs={{0,64},{1,65},{2,66},{3,67},{4,68},{5,69},{6,70},{7,71},{8,72},{9,... | collective-permute-start | bytes 61448 | tf_op jit(solution)/shard_map/ppermute | solution.py:244
  63.2 5.0 %collective-permute-start.8 = (f32[40,128]{1,0:T(8,128)S(1)}, f32[40,128]{1,0:T(8,128)S(1)}, u32[]{:S(2)}, u32[]{:S(2)}) collective-permute-start(f32[40,128]{1,0:T(8,128)S(1)} %add_add_fusion.2), channel_id=1, source_target_pairs={{0,32},{1,33},{2,34},{3,35},{4,36},{5,37},{6,38},{7,39},{8,40},{9,... | collective-permute-start | bytes 61448 | tf_op jit(solution)/shard_map/ppermute | solution.py:244
  63.9 4.2 %collective-permute-start.9 = (f32[40,128]{1,0:T(8,128)S(1)}, f32[40,128]{1,0:T(8,128)S(1)}, u32[]{:S(2)}, u32[]{:S(2)}) collective-permute-start(f32[40,128]{1,0:T(8,128)S(1)} %add_add_fusion.2), channel_id=1, source_target_pairs={{0,96},{1,97},{2,98},{3,99},{4,100},{5,101},{6,102},{7,103},{8,104... | collective-permute-start | bytes 61448 | tf_op jit(solution)/shard_map/ppermute | solution.py:244
  68.2 3.9 %collective-permute-start.11 = (f32[40,128]{1,0:T(8,128)S(1)}, f32[40,128]{1,0:T(8,128)S(1)}, u32[]{:S(2)}, u32[]{:S(2)}) collective-permute-start(f32[40,128]{1,0:T(8,128)S(1)} %add_add_fusion.1), channel_id=1, source_target_pairs={{0,4},{1,5},{2,6},{3,7},{4,8},{5,9},{6,10},{7,11},{8,12},{9,13},{1... | collective-permute-start | bytes 61448 | tf_op jit(solution)/shard_map/ppermute | solution.py:244
  68.3 3.8 %collective-permute-start.12 = (f32[40,128]{1,0:T(8,128)S(1)}, f32[40,128]{1,0:T(8,128)S(1)}, u32[]{:S(2)}, u32[]{:S(2)}) collective-permute-start(f32[40,128]{1,0:T(8,128)S(1)} %add_add_fusion.1), channel_id=1, source_target_pairs={{0,28},{1,29},{2,30},{3,31},{4,0},{5,1},{6,2},{7,3},{8,4},{9,5},{1... | collective-permute-start | bytes 61448 | tf_op jit(solution)/shard_map/ppermute | solution.py:244
  70.3 5.9 %collective-permute-start.13 = (f32[40,128]{1,0:T(8,128)S(1)}, f32[40,128]{1,0:T(8,128)S(1)}, u32[]{:S(2)}, u32[]{:S(2)}) collective-permute-start(f32[40,128]{1,0:T(8,128)S(1)} %add_add_fusion.1), channel_id=1, source_target_pairs={{0,8},{1,9},{2,10},{3,11},{4,12},{5,13},{6,14},{7,15},{8,16},{9,17... | collective-permute-start | bytes 61448 | tf_op jit(solution)/shard_map/ppermute | solution.py:244
  76.2 1.5 %collective-permute-start.14 = (f32[40,128]{1,0:T(8,128)S(1)}, f32[40,128]{1,0:T(8,128)S(1)}, u32[]{:S(2)}, u32[]{:S(2)}) collective-permute-start(f32[40,128]{1,0:T(8,128)S(1)} %add_add_fusion.mine), channel_id=1, source_target_pairs={{0,128},{128,0},{1,129},{129,1},{2,130},{130,2},{3,131},{131,3},{4... | collective-permute-start | bytes 61448 | tf_op jit(solution)/shard_map/ppermute | solution.py:230

commit v5 on v3

--- a/solution.py
+++ b/solution.py
@@ -100,15 +100,17 @@
     ]
     cov_sum = jnp.where(live, plain(cov) + plain(cov_peer), 0.0)
     cov_parts = parts(pad_rows(cov_sum, 16))
-    left = jnp.concatenate([*pick, *cov_parts], axis=0)
+    cov_left = jnp.concatenate(cov_parts, axis=0)
+    left = jnp.concatenate([*pick, cov_left], axis=0)
     mcf_left = jnp.concatenate(parts(pad_rows(plain(mcf) + plain(mcf_peer), 16)), axis=0)
     table = coef[...]
     base = 2 * LANES
     for pair in range(chunks // 2):
         cols = pl.ds(pair * base, base)
-        got = sum(mm(left, piece, NT) for piece in halves(geno[0, cols, :]))
-        masked = sum(mm(mcf_left, piece, NT) for piece in halves(mg[0, cols, :]))
-        grams = got[base:] - masked
+        g_high, g_mid, g_low = parts(geno[0, cols, :])
+        got = mm(left, g_high, NT) + mm(left, g_mid, NT)
+        masked = sum(mm(mcf_left, piece, NT) for piece in parts(mg[0, cols, :]))
+        grams = got[base:] + mm(cov_left, g_low, NT) - masked
         grams = grams[:16] + grams[16:32] + grams[32:48]
         for part in range(2):
             c = 2 * pair + part
@@ -200,7 +202,10 @@
         )
         r_high, r_mid = halves(values)
         payload[pl.ds(8 + half, owners, stride=out_rows), :] = (
-            mm(r_high, p_mid, NT) + mm(r_mid, p_high, NT) + mm(r_high, p_high, NT)
+            mm(r_mid, p_mid, NT)
+            + mm(r_high, p_mid, NT)
+            + mm(r_mid, p_high, NT)
+            + mm(r_high, p_high, NT)
         )
 
 

time: 106 us -> 106 us (level)
  no operation moved by 1% of the time
where the time goes in v5:
time: 106 us
  waiting for transfers between devices  37.9 us (36%)
  starting transfers between devices  34.6 us (33%)
  blocking collectives  27.1 us (26%)
  Pallas kernels  5.75 us (5%)
    ppermute x10, waiting for transfers between devices, shifted(): return lax.ppermute(value, 'smp', pairs)  37.1 us
    all_to_all x1, blocking collectives, exchange(): got = lax.all_to_all(flat, 'smp', split_axis=0, concat_axis=0, tiled=True)  27.1 us
    ppermute x10, starting transfers between devices, shifted(): return lax.ppermute(value, 'smp', pairs)  18.4 us
    all_to_all x1, starting transfers between devices, exchange(): got = lax.all_to_all(flat, 'smp', split_axis=0, concat_axis=0, tiled=True)  15.1 us
    pallas_call x1, Pallas kernels, local(): pl.pallas_call(pack_kernel, out_shape=(jax.ShapeDtypeStruct((peers * (2 *...  2.14 us
  transfers between devices with their start and end apart: 15, of which 9 were waited for; matrix products, arithmetic and copies ran while one was open for 0% of the time, Pallas kernels for 1%

profile of v5, /device:TPU:32, one launch (start us, length us, event | category | flops | bytes accessed | tf_op | source)
XLA Modules:
  0.0 106.2 jit_solution(3735439089468826015)
XLA Ops:
  0.6 0.1 collective-permute-start
  0.7 0.5 collective-permute-start.1
  1.2 1.5 %shard_map.122 = (s32[1,256]{1,0:T(1,128)S(1)}, f32[1,1024,256]{2,1,0:T(8,128)S(1)}, f32[10,1,256]{2,1,0:T(1,128)S(1)}, f32[10,1,128]{2,1,0:T(1,128)S(1)}, f32[1...) custom-call(s32[1,256]{1,0:T(1,128)} %bitcast.24, ...), custom_call_target="tpu_custom_call" | custom-call | tf_op jit(solution)/shard_map/pallas_call | solution.py:65
  2.7 0.0 collective-permute-done.1.mcf_peer
  2.7 0.0 collective-permute-done.cov_peer
  2.7 2.1 %shard_map.123 = (f32[2176,128]{1,0:T(8,128)}, f32[80,128]{1,0:T(8,128)S(1)}) custom-call(s32[1,256]{1,0:T(1,128)S(1)} %get-tuple-element.14.ids, f32[1,1024,256]{2,1,0:T(8,128)S(1)} %get-tuple-element.15.geno, f32[10,1,256]{2,1,0:T(1,128)S(1)} %get-tuple-element.16.cov, f32[10,1,256]{2,1,0:T(1,128)S(1)} %collective-permute-done.cov_peer, ...), custom_call_target="tpu_custom_call" | custom-call | tf_op jit(solution)/shard_map/pallas_call | solution.py:290
  4.9 15.1 %all-to-all-start = ((f32[128,1,2176]{2,1,0:T(1,128)}), f32[128,1,2176]{2,1,0:T(1,128)S(1)}, u32[]{:S(2)}, u32[]{:S(2)}) async-start(f32[128,1,2176]{2,1,0:T(1,128)} %bitcast.5), calls=%async_computation | async-start | bytes 2228224 | tf_op jit(solution)/shard_map/all_to_all | solution.py:262
  20.0 4.6 %collective-permute-start.2 = (f32[80,128]{1,0:T(8,128)S(1)}, f32[80,128]{1,0:T(8,128)S(1)}, u32[]{:S(2)}, u32[]{:S(2)}) collective-permute-start(f32[80,128]{1,0:T(8,128)S(1)} %get-tuple-element.23), channel_id=1, source_target_pairs={{0,16},{1,17},{2,18},{3,19},{4,20},{5,21},{6,22},{7,23},{8,24},{9,... | collective-permute-start | bytes 122888 | tf_op jit(solution)/shard_map/ppermute | solution.py:240
  24.6 25.3 %collective-permute-done.2 = f32[80,128]{1,0:T(8,128)S(1)} collective-permute-done((f32[80,128]{1,0:T(8,128)S(1)}, f32[80,128]{1,0:T(8,128)S(1)}, u32[]{:S(2)}, u32[]{:S(2)}) %collective-permute-start.2) | collective-permute-done | bytes 40992 | tf_op jit(solution)/shard_map/ppermute | solution.py:240
  49.9 0.0 collective-permute-start.3
  49.9 0.5 collective-permute-start.4
  50.4 0.7 collective-permute-done.3
  51.1 0.1 collective-permute-done.4.mcs_peer
  51.2 1.5 %collective-permute-start.5 = (f32[80,128]{1,0:T(8,128)S(1)}, f32[80,128]{1,0:T(8,128)S(1)}, u32[]{:S(2)}, u32[]{:S(2)}) collective-permute-start(f32[80,128]{1,0:T(8,128)S(1)} %add.25), channel_id=1, source_target_pairs={{0,1},{1,2},{2,3},{3,0},{4,5},{5,6},{6,7},{7,4},{8,9},{9,10},{10,1... | collective-permute-start | bytes 122888 | tf_op jit(solution)/shard_map/ppermute | solution.py:240
  52.7 1.8 %collective-permute-start.6 = (f32[80,128]{1,0:T(8,128)S(1)}, f32[80,128]{1,0:T(8,128)S(1)}, u32[]{:S(2)}, u32[]{:S(2)}) collective-permute-start(f32[80,128]{1,0:T(8,128)S(1)} %add.25), channel_id=1, source_target_pairs={{0,3},{1,0},{2,1},{3,2},{4,7},{5,4},{6,5},{7,6},{8,11},{9,8},{10,9... | collective-permute-start | bytes 122888 | tf_op jit(solution)/shard_map/ppermute | solution.py:240
  54.5 1.8 %collective-permute-start.7 = (f32[80,128]{1,0:T(8,128)S(1)}, f32[80,128]{1,0:T(8,128)S(1)}, u32[]{:S(2)}, u32[]{:S(2)}) collective-permute-start(f32[80,128]{1,0:T(8,128)S(1)} %add.25), channel_id=1, source_target_pairs={{0,2},{1,3},{2,0},{3,1},{4,6},{5,7},{6,4},{7,5},{8,10},{9,11},{10,... | collective-permute-start | bytes 122888 | tf_op jit(solution)/shard_map/ppermute | solution.py:240
  56.2 0.2 collective-permute-done.5
  56.5 0.3 collective-permute-done.6
  56.7 3.3 %collective-permute-done.7 = f32[80,128]{1,0:T(8,128)S(1)} collective-permute-done((f32[80,128]{1,0:T(8,128)S(1)}, f32[80,128]{1,0:T(8,128)S(1)}, u32[]{:S(2)}, u32[]{:S(2)}) %collective-permute-start.7) | collective-permute-done | bytes 40992 | tf_op jit(solution)/shard_map/ppermute | solution.py:240
  60.0 3.5 %collective-permute-start.10 = (f32[80,128]{1,0:T(8,128)S(1)}, f32[80,128]{1,0:T(8,128)S(1)}, u32[]{:S(2)}, u32[]{:S(2)}) collective-permute-start(f32[80,128]{1,0:T(8,128)S(1)} %add_add_fusion.1), channel_id=1, source_target_pairs={{0,64},{1,65},{2,66},{3,67},{4,68},{5,69},{6,70},{7,71},{8,72},{9,... | collective-permute-start | bytes 122888 | tf_op jit(solution)/shard_map/ppermute | solution.py:240
  63.5 0.8 collective-permute-start.8
  64.3 2.5 %collective-permute-start.9 = (f32[80,128]{1,0:T(8,128)S(1)}, f32[80,128]{1,0:T(8,128)S(1)}, u32[]{:S(2)}, u32[]{:S(2)}) collective-permute-start(f32[80,128]{1,0:T(8,128)S(1)} %add_add_fusion.1), channel_id=1, source_target_pairs={{0,96},{1,97},{2,98},{3,99},{4,100},{5,101},{6,102},{7,103},{8,104... | collective-permute-start | bytes 122888 | tf_op jit(solution)/shard_map/ppermute | solution.py:240
  66.7 0.0 collective-permute-done.10
  66.7 2.0 %collective-permute-done.8 = f32[80,128]{1,0:T(8,128)S(1)} collective-permute-done((f32[80,128]{1,0:T(8,128)S(1)}, f32[80,128]{1,0:T(8,128)S(1)}, u32[]{:S(2)}, u32[]{:S(2)}) %collective-permute-start.8) | collective-permute-done | bytes 40992 | tf_op jit(solution)/shard_map/ppermute | solution.py:240
  68.7 0.1 collective-permute-start.11
  68.9 2.0 %collective-permute-start.12 = (f32[80,128]{1,0:T(8,128)S(1)}, f32[80,128]{1,0:T(8,128)S(1)}, u32[]{:S(2)}, u32[]{:S(2)}) collective-permute-start(f32[80,128]{1,0:T(8,128)S(1)} %add_add_fusion.w_0), channel_id=1, source_target_pairs={{0,28},{1,29},{2,30},{3,31},{4,0},{5,1},{6,2},{7,3},{8,4},{9,5},{1... | collective-permute-start | bytes 122888 | tf_op jit(solution)/shard_map/ppermute | solution.py:240
  70.8 0.0 collective-permute-start.13
  70.8 2.3 %collective-permute-done.11.w_1 = f32[80,128]{1,0:T(8,128)S(1)} collective-permute-done((f32[80,128]{1,0:T(8,128)S(1)}, f32[80,128]{1,0:T(8,128)S(1)}, u32[]{:S(2)}, u32[]{:S(2)}) %collective-permute-start.11) | collective-permute-done | bytes 40992 | tf_op jit(solution)/shard_map/ppermute | solution.py:240
  73.1 3.8 %collective-permute-done.13.w_3 = f32[80,128]{1,0:T(8,128)S(1)} collective-permute-done((f32[80,128]{1,0:T(8,128)S(1)}, f32[80,128]{1,0:T(8,128)S(1)}, u32[]{:S(2)}, u32[]{:S(2)}) %collective-permute-start.13) | collective-permute-done | bytes 40992 | tf_op jit(solution)/shard_map/ppermute | solution.py:240
  77.0 1.3 %shard_map.124 = f32[1280,128]{1,0:T(8,128)S(1)} custom-call(f32[2176,128]{1,0:T(8,128)S(1)} %bitcast.11, f32[80,128]{1,0:T(8,128)S(1)} %add_add_fusion.w_0, f32[80,128]{1,0:T(8,128)S(1)} %collective-permute-done.11.w_1, f32[80,128]{1,0:T(8,128)S(1)} %collective-permute-done.12.w_2, f32[80,128]{1,0:T(8,128)S(1)} %collective-permute-done.13.w_3, ...), custom_call_target="tpu_custom_call" | custom-call | tf_op jit(solution)/shard_map/pallas_call | solution.py:309
  78.3 27.1 %all_to_all.10 = f32[128,1,1280]{2,1,0:T(1,128)S(1)} all-to-all(f32[128,1,1280]{2,1,0:T(1,128)S(1)} %bitcast.13), channel_id=1, replica_groups=mesh['srv'=2,'smp'=128] {'smp'}, dimensions={0} | all-to-all | bytes 1310720 | tf_op jit(solution)/shard_map/all_to_all | solution.py:262
  105.3 0.8 shard_map.125
  (15 shorter events, 0.1 us)
Async XLA Ops:
  0.6 2.1 %collective-permute-start = (f32[10,1,256]{2,1,0:T(1,128)}, f32[10,1,256]{2,1,0:T(1,128)S(1)}, u32[]{:S(2)}, u32[]{:S(2)}) collective-permute-start(f32[10,1,256]{2,1,0:T(1,128)} %bitcast.20), channel_id=1, source_target_pairs={{0,128},{128,0},{1,129},{129,1},{2,130},{130,2},{3,131},{131,3},{4... | collective-permute-start | bytes 30728 | tf_op jit(solution)/shard_map/ppermute | solution.py:226
  0.7 2.0 %collective-permute-start.1 = (f32[10,1,128]{2,1,0:T(1,128)}, f32[10,1,128]{2,1,0:T(1,128)S(1)}, u32[]{:S(2)}, u32[]{:S(2)}) collective-permute-start(f32[10,1,128]{2,1,0:T(1,128)} %bitcast.22), channel_id=1, source_target_pairs={{0,128},{128,0},{1,129},{129,1},{2,130},{130,2},{3,131},{131,3},{4... | collective-permute-start | bytes 15368 | tf_op jit(solution)/shard_map/ppermute | solution.py:226
  4.9 45.0 %copy-start.3 = (f32[1,10,128]{2,0,1:T(1,128)S(1)}, f32[1,10,128]{2,0,1:T(1,128)}, u32[]{:S(2)}) copy-start(f32[1,10,128]{2,0,1:T(1,128)} %param.17) | copy-start | bytes 15364
  4.9 72.1 %copy-start = (f32[1,1024,128]{2,1,0:T(8,128)S(1)}, f32[1,1024,128]{2,1,0:T(8,128)}, u32[]{:S(2)}) copy-start(f32[1,1024,128]{2,1,0:T(8,128)} %prod_second.1) | copy-start | bytes 1572868
  4.9 72.1 %copy-start.1 = (f32[1,10,1024]{2,0,1:T(1,128)S(1)}, f32[1,10,1024]{2,0,1:T(1,128)}, u32[]{:S(2)}) copy-start(f32[1,10,1024]{2,0,1:T(1,128)} %param.18) | copy-start | bytes 122884
  4.9 72.1 %copy-start.2 = (f32[128,32]{0,1:T(8,128)S(1)}, f32[128,32]{0,1:T(8,128)}, u32[]{:S(2)}) copy-start(f32[128,32]{0,1:T(8,128)} %param.21) | copy-start | bytes 49156
  4.9 72.0 %all-to-all-start = ((f32[128,1,2176]{2,1,0:T(1,128)}), f32[128,1,2176]{2,1,0:T(1,128)S(1)}, u32[]{:S(2)}, u32[]{:S(2)}) async-start(f32[128,1,2176]{2,1,0:T(1,128)} %bitcast.5), calls=%async_computation | async-start | bytes 2228224 | tf_op jit(solution)/shard_map/all_to_all | solution.py:262
  20.0 29.8 %collective-permute-start.2 = (f32[80,128]{1,0:T(8,128)S(1)}, f32[80,128]{1,0:T(8,128)S(1)}, u32[]{:S(2)}, u32[]{:S(2)}) collective-permute-start(f32[80,128]{1,0:T(8,128)S(1)} %get-tuple-element.23), channel_id=1, source_target_pairs={{0,16},{1,17},{2,18},{3,19},{4,20},{5,21},{6,22},{7,23},{8,24},{9,... | collective-permute-start | bytes 122888 | tf_op jit(solution)/shard_map/ppermute | solution.py:240
  49.9 1.2 %collective-permute-start.3 = (f32[80,128]{1,0:T(8,128)S(1)}, f32[80,128]{1,0:T(8,128)S(1)}, u32[]{:S(2)}, u32[]{:S(2)}) collective-permute-start(f32[80,128]{1,0:T(8,128)S(1)} %add.24), channel_id=1, source_target_pairs={{0,128},{128,0},{1,129},{129,1},{2,130},{130,2},{3,131},{131,3},{4... | collective-permute-start | bytes 122888 | tf_op jit(solution)/shard_map/ppermute | solution.py:226
  49.9 1.3 %collective-permute-start.4 = (f32[10,1,128]{2,1,0:T(1,128)S(1)}, f32[10,1,128]{2,1,0:T(1,128)S(1)}, u32[]{:S(2)}, u32[]{:S(2)}) collective-permute-start(f32[10,1,128]{2,1,0:T(1,128)S(1)} %bitcast.17), channel_id=1, source_target_pairs={{0,128},{128,0},{1,129},{129,1},{2,130},{130,2},{3,131},{131,3},{4... | collective-permute-start | bytes 15368 | tf_op jit(solution)/shard_map/ppermute | solution.py:226
  51.2 5.2 %collective-permute-start.5 = (f32[80,128]{1,0:T(8,128)S(1)}, f32[80,128]{1,0:T(8,128)S(1)}, u32[]{:S(2)}, u32[]{:S(2)}) collective-permute-start(f32[80,128]{1,0:T(8,128)S(1)} %add.25), channel_id=1, source_target_pairs={{0,1},{1,2},{2,3},{3,0},{4,5},{5,6},{6,7},{7,4},{8,9},{9,10},{10,1... | collective-permute-start | bytes 122888 | tf_op jit(solution)/shard_map/ppermute | solution.py:240
  52.7 4.0 %collective-permute-start.6 = (f32[80,128]{1,0:T(8,128)S(1)}, f32[80,128]{1,0:T(8,128)S(1)}, u32[]{:S(2)}, u32[]{:S(2)}) collective-permute-start(f32[80,128]{1,0:T(8,128)S(1)} %add.25), channel_id=1, source_target_pairs={{0,3},{1,0},{2,1},{3,2},{4,7},{5,4},{6,5},{7,6},{8,11},{9,8},{10,9... | collective-permute-start | bytes 122888 | tf_op jit(solution)/shard_map/ppermute | solution.py:240
  54.5 5.5 %collective-permute-start.7 = (f32[80,128]{1,0:T(8,128)S(1)}, f32[80,128]{1,0:T(8,128)S(1)}, u32[]{:S(2)}, u32[]{:S(2)}) collective-permute-start(f32[80,128]{1,0:T(8,128)S(1)} %add.25), channel_id=1, source_target_pairs={{0,2},{1,3},{2,0},{3,1},{4,6},{5,7},{6,4},{7,5},{8,10},{9,11},{10,... | collective-permute-start | bytes 122888 | tf_op jit(solution)/shard_map/ppermute | solution.py:240
  60.0 6.7 %collective-permute-start.10 = (f32[80,128]{1,0:T(8,128)S(1)}, f32[80,128]{1,0:T(8,128)S(1)}, u32[]{:S(2)}, u32[]{:S(2)}) collective-permute-start(f32[80,128]{1,0:T(8,128)S(1)} %add_add_fusion.1), channel_id=1, source_target_pairs={{0,64},{1,65},{2,66},{3,67},{4,68},{5,69},{6,70},{7,71},{8,72},{9,... | collective-permute-start | bytes 122888 | tf_op jit(solution)/shard_map/ppermute | solution.py:240
  63.5 5.2 %collective-permute-start.8 = (f32[80,128]{1,0:T(8,128)S(1)}, f32[80,128]{1,0:T(8,128)S(1)}, u32[]{:S(2)}, u32[]{:S(2)}) collective-permute-start(f32[80,128]{1,0:T(8,128)S(1)} %add_add_fusion.1), channel_id=1, source_target_pairs={{0,32},{1,33},{2,34},{3,35},{4,36},{5,37},{6,38},{7,39},{8,40},{9,... | collective-permute-start | bytes 122888 | tf_op jit(solution)/shard_map/ppermute | solution.py:240
  64.3 4.4 %collective-permute-start.9 = (f32[80,128]{1,0:T(8,128)S(1)}, f32[80,128]{1,0:T(8,128)S(1)}, u32[]{:S(2)}, u32[]{:S(2)}) collective-permute-start(f32[80,128]{1,0:T(8,128)S(1)} %add_add_fusion.1), channel_id=1, source_target_pairs={{0,96},{1,97},{2,98},{3,99},{4,100},{5,101},{6,102},{7,103},{8,104... | collective-permute-start | bytes 122888 | tf_op jit(solution)/shard_map/ppermute | solution.py:240
  68.7 4.4 %collective-permute-start.11 = (f32[80,128]{1,0:T(8,128)S(1)}, f32[80,128]{1,0:T(8,128)S(1)}, u32[]{:S(2)}, u32[]{:S(2)}) collective-permute-start(f32[80,128]{1,0:T(8,128)S(1)} %add_add_fusion.w_0), channel_id=1, source_target_pairs={{0,4},{1,5},{2,6},{3,7},{4,8},{5,9},{6,10},{7,11},{8,12},{9,13},{1... | collective-permute-start | bytes 122888 | tf_op jit(solution)/shard_map/ppermute | solution.py:240
  68.9 4.2 %collective-permute-start.12 = (f32[80,128]{1,0:T(8,128)S(1)}, f32[80,128]{1,0:T(8,128)S(1)}, u32[]{:S(2)}, u32[]{:S(2)}) collective-permute-start(f32[80,128]{1,0:T(8,128)S(1)} %add_add_fusion.w_0), channel_id=1, source_target_pairs={{0,28},{1,29},{2,30},{3,31},{4,0},{5,1},{6,2},{7,3},{8,4},{9,5},{1... | collective-permute-start | bytes 122888 | tf_op jit(solution)/shard_map/ppermute | solution.py:240
  70.8 6.1 %collective-permute-start.13 = (f32[80,128]{1,0:T(8,128)S(1)}, f32[80,128]{1,0:T(8,128)S(1)}, u32[]{:S(2)}, u32[]{:S(2)}) collective-permute-start(f32[80,128]{1,0:T(8,128)S(1)} %add_add_fusion.w_0), channel_id=1, source_target_pairs={{0,8},{1,9},{2,10},{3,11},{4,12},{5,13},{6,14},{7,15},{8,16},{9,17... | collective-permute-start | bytes 122888 | tf_op jit(solution)/shard_map/ppermute | solution.py:240

commit v6 on v5

--- a/solution.py
+++ b/solution.py
@@ -303,9 +303,9 @@
     weight = weight + swap(weight)
     mcs_peer = swap(mcs)
     weight, mcs_peer = lax.optimization_barrier((weight, mcs_peer))
-    weight = total(terms(weight, (0, 0, 1), (0, 0, 3), (0, 0, 2)))
-    weight = total(terms(weight, (1, 0, 0), (3, 0, 0), (2, 0, 0)))
-    open_weight = terms(weight, (0, 1, 0), (0, 7, 0), (0, 2, 0))
+    weight = total(terms(weight, (0, 0, 2), (0, 0, 1), (0, 0, 3)))
+    weight = total(terms(weight, (2, 0, 0), (1, 0, 0), (3, 0, 0)))
+    open_weight = terms(weight, (0, 2, 0), (0, 1, 0), (0, 7, 0))
     fitted = pl.pallas_call(
         fit_kernel,
         out_shape=jax.ShapeDtypeStruct((variants // 8 * 10, LANES), jnp.float32),

time: 106 us -> 106 us (level)
  waiting for transfers between devices: 37.9 us -> 36.5 us
  blocking collectives: 27.1 us -> 28.2 us
    ppermute x10, waiting for transfers between devices: 37.1 us -> 35.7 us  [shifted(): return lax.ppermute(value, 'smp', pairs)]
    all_to_all x1, blocking collectives: 27.1 us -> 28.2 us  [exchange(): got = lax.all_to_all(flat, 'smp', split_axis=0, concat_axis=0, tiled=True)]
  transfers between devices with their start and end apart: 15 -> 15, of which waited for: 9 -> 8; matrix products, arithmetic and copies ran while one was open for 0% -> 0% of each run, Pallas kernels for 1% -> 1%
where the time goes in v6:
time: 106 us; the launch traced here: 105 us
  waiting for transfers between devices  36.5 us (34%)
  starting transfers between devices  34.1 us (32%)
  blocking collectives  28.2 us (27%)
  Pallas kernels  5.74 us (5%)
    ppermute x10, waiting for transfers between devices, shifted(): return lax.ppermute(value, 'smp', pairs)  35.7 us
    all_to_all x1, blocking collectives, exchange(): got = lax.all_to_all(flat, 'smp', split_axis=0, concat_axis=0, tiled=True)  28.2 us
    ppermute x10, starting transfers between devices, shifted(): return lax.ppermute(value, 'smp', pairs)  17.9 us
    all_to_all x1, starting transfers between devices, exchange(): got = lax.all_to_all(flat, 'smp', split_axis=0, concat_axis=0, tiled=True)  15.1 us
    pallas_call x1, Pallas kernels, local(): pl.pallas_call(pack_kernel, out_shape=(jax.ShapeDtypeStruct((peers * (2 *...  2.14 us
  transfers between devices with their start and end apart: 15, of which 8 were waited for; matrix products, arithmetic and copies ran while one was open for 0% of the time, Pallas kernels for 1%

profile of v6, /device:TPU:32, one launch (start us, length us, event | category | flops | bytes accessed | tf_op | source)
XLA Modules:
  0.0 105.4 jit_solution(15746170727765105960)
XLA Ops:
  0.6 0.1 collective-permute-start
  0.7 0.5 collective-permute-start.1
  1.2 1.5 %shard_map.122 = (s32[1,256]{1,0:T(1,128)S(1)}, f32[1,1024,256]{2,1,0:T(8,128)S(1)}, f32[10,1,256]{2,1,0:T(1,128)S(1)}, f32[10,1,128]{2,1,0:T(1,128)S(1)}, f32[1...) custom-call(s32[1,256]{1,0:T(1,128)} %bitcast.24, ...), custom_call_target="tpu_custom_call" | custom-call | tf_op jit(solution)/shard_map/pallas_call | solution.py:65
  2.7 0.0 collective-permute-done.1.mcf_peer
  2.7 0.0 collective-permute-done.cov_peer
  2.7 2.1 %shard_map.123 = (f32[2176,128]{1,0:T(8,128)}, f32[80,128]{1,0:T(8,128)S(1)}) custom-call(s32[1,256]{1,0:T(1,128)S(1)} %get-tuple-element.14.ids, f32[1,1024,256]{2,1,0:T(8,128)S(1)} %get-tuple-element.15.geno, f32[10,1,256]{2,1,0:T(1,128)S(1)} %get-tuple-element.16.cov, f32[10,1,256]{2,1,0:T(1,128)S(1)} %collective-permute-done.cov_peer, ...), custom_call_target="tpu_custom_call" | custom-call | tf_op jit(solution)/shard_map/pallas_call | solution.py:290
  4.9 15.1 %all-to-all-start = ((f32[128,1,2176]{2,1,0:T(1,128)}), f32[128,1,2176]{2,1,0:T(1,128)S(1)}, u32[]{:S(2)}, u32[]{:S(2)}) async-start(f32[128,1,2176]{2,1,0:T(1,128)} %bitcast.5), calls=%async_computation | async-start | bytes 2228224 | tf_op jit(solution)/shard_map/all_to_all | solution.py:262
  20.0 4.6 %collective-permute-start.2 = (f32[80,128]{1,0:T(8,128)S(1)}, f32[80,128]{1,0:T(8,128)S(1)}, u32[]{:S(2)}, u32[]{:S(2)}) collective-permute-start(f32[80,128]{1,0:T(8,128)S(1)} %get-tuple-element.23), channel_id=1, source_target_pairs={{0,16},{1,17},{2,18},{3,19},{4,20},{5,21},{6,22},{7,23},{8,24},{9,... | collective-permute-start | bytes 122888 | tf_op jit(solution)/shard_map/ppermute | solution.py:240
  24.6 25.3 %collective-permute-done.2 = f32[80,128]{1,0:T(8,128)S(1)} collective-permute-done((f32[80,128]{1,0:T(8,128)S(1)}, f32[80,128]{1,0:T(8,128)S(1)}, u32[]{:S(2)}, u32[]{:S(2)}) %collective-permute-start.2) | collective-permute-done | bytes 40992 | tf_op jit(solution)/shard_map/ppermute | solution.py:240
  49.9 0.0 collective-permute-start.3
  49.9 0.5 collective-permute-start.4
  50.4 0.7 collective-permute-done.3
  51.1 0.1 collective-permute-done.4.mcs_peer
  51.2 3.0 %collective-permute-start.5 = (f32[80,128]{1,0:T(8,128)S(1)}, f32[80,128]{1,0:T(8,128)S(1)}, u32[]{:S(2)}, u32[]{:S(2)}) collective-permute-start(f32[80,128]{1,0:T(8,128)S(1)} %add.25), channel_id=1, source_target_pairs={{0,2},{1,3},{2,0},{3,1},{4,6},{5,7},{6,4},{7,5},{8,10},{9,11},{10,... | collective-permute-start | bytes 122888 | tf_op jit(solution)/shard_map/ppermute | solution.py:240
  54.2 0.6 collective-permute-start.6
  54.8 2.7 %collective-permute-start.7 = (f32[80,128]{1,0:T(8,128)S(1)}, f32[80,128]{1,0:T(8,128)S(1)}, u32[]{:S(2)}, u32[]{:S(2)}) collective-permute-start(f32[80,128]{1,0:T(8,128)S(1)} %add.25), channel_id=1, source_target_pairs={{0,3},{1,0},{2,1},{3,2},{4,7},{5,4},{6,5},{7,6},{8,11},{9,8},{10,9... | collective-permute-start | bytes 122888 | tf_op jit(solution)/shard_map/ppermute | solution.py:240
  57.5 2.0 %collective-permute-done.6 = f32[80,128]{1,0:T(8,128)S(1)} collective-permute-done((f32[80,128]{1,0:T(8,128)S(1)}, f32[80,128]{1,0:T(8,128)S(1)}, u32[]{:S(2)}, u32[]{:S(2)}) %collective-permute-start.6) | collective-permute-done | bytes 40992 | tf_op jit(solution)/shard_map/ppermute | solution.py:240
  59.4 0.0 collective-permute-done.7
  59.5 3.4 %collective-permute-start.10 = (f32[80,128]{1,0:T(8,128)S(1)}, f32[80,128]{1,0:T(8,128)S(1)}, u32[]{:S(2)}, u32[]{:S(2)}) collective-permute-start(f32[80,128]{1,0:T(8,128)S(1)} %add_add_fusion.1), channel_id=1, source_target_pairs={{0,96},{1,97},{2,98},{3,99},{4,100},{5,101},{6,102},{7,103},{8,104... | collective-permute-start | bytes 122888 | tf_op jit(solution)/shard_map/ppermute | solution.py:240
  62.9 0.4 collective-permute-start.8
  63.3 1.1 %collective-permute-start.9 = (f32[80,128]{1,0:T(8,128)S(1)}, f32[80,128]{1,0:T(8,128)S(1)}, u32[]{:S(2)}, u32[]{:S(2)}) collective-permute-start(f32[80,128]{1,0:T(8,128)S(1)} %add_add_fusion.1), channel_id=1, source_target_pairs={{0,32},{1,33},{2,34},{3,35},{4,36},{5,37},{6,38},{7,39},{8,40},{9,... | collective-permute-start | bytes 122888 | tf_op jit(solution)/shard_map/ppermute | solution.py:240
  64.4 0.2 collective-permute-done.10
  64.5 3.9 %collective-permute-done.8 = f32[80,128]{1,0:T(8,128)S(1)} collective-permute-done((f32[80,128]{1,0:T(8,128)S(1)}, f32[80,128]{1,0:T(8,128)S(1)}, u32[]{:S(2)}, u32[]{:S(2)}) %collective-permute-start.8) | collective-permute-done | bytes 40992 | tf_op jit(solution)/shard_map/ppermute | solution.py:240
  68.4 0.4 collective-permute-done.9
  68.8 0.1 collective-permute-start.11
  68.9 0.1 collective-permute-start.12
  69.0 2.0 %collective-permute-start.13 = (f32[80,128]{1,0:T(8,128)S(1)}, f32[80,128]{1,0:T(8,128)S(1)}, u32[]{:S(2)}, u32[]{:S(2)}) collective-permute-start(f32[80,128]{1,0:T(8,128)S(1)} %add_add_fusion.w_0), channel_id=1, source_target_pairs={{0,28},{1,29},{2,30},{3,31},{4,0},{5,1},{6,2},{7,3},{8,4},{9,5},{1... | collective-permute-start | bytes 122888 | tf_op jit(solution)/shard_map/ppermute | solution.py:240
  71.0 4.0 %collective-permute-done.11.w_1 = f32[80,128]{1,0:T(8,128)S(1)} collective-permute-done((f32[80,128]{1,0:T(8,128)S(1)}, f32[80,128]{1,0:T(8,128)S(1)}, u32[]{:S(2)}, u32[]{:S(2)}) %collective-permute-start.11) | collective-permute-done | bytes 40992 | tf_op jit(solution)/shard_map/ppermute | solution.py:240
  75.0 0.0 all-to-all-done
  75.0 1.3 %shard_map.124 = f32[1280,128]{1,0:T(8,128)S(1)} custom-call(f32[2176,128]{1,0:T(8,128)S(1)} %bitcast.11, f32[80,128]{1,0:T(8,128)S(1)} %add_add_fusion.w_0, f32[80,128]{1,0:T(8,128)S(1)} %collective-permute-done.11.w_1, f32[80,128]{1,0:T(8,128)S(1)} %collective-permute-done.12.w_2, f32[80,128]{1,0:T(8,128)S(1)} %collective-permute-done.13.w_3, ...), custom_call_target="tpu_custom_call" | custom-call | tf_op jit(solution)/shard_map/pallas_call | solution.py:309
  76.3 28.2 %all_to_all.10 = f32[128,1,1280]{2,1,0:T(1,128)S(1)} all-to-all(f32[128,1,1280]{2,1,0:T(1,128)S(1)} %bitcast.13), channel_id=1, replica_groups=mesh['srv'=2,'smp'=128] {'smp'}, dimensions={0} | all-to-all | bytes 1310720 | tf_op jit(solution)/shard_map/all_to_all | solution.py:262
  104.5 0.8 shard_map.125
  (15 shorter events, 0.1 us)
Async XLA Ops:
  0.6 2.1 %collective-permute-start = (f32[10,1,256]{2,1,0:T(1,128)}, f32[10,1,256]{2,1,0:T(1,128)S(1)}, u32[]{:S(2)}, u32[]{:S(2)}) collective-permute-start(f32[10,1,256]{2,1,0:T(1,128)} %bitcast.20), channel_id=1, source_target_pairs={{0,128},{128,0},{1,129},{129,1},{2,130},{130,2},{3,131},{131,3},{4... | collective-permute-start | bytes 30728 | tf_op jit(solution)/shard_map/ppermute | solution.py:226
  0.7 2.0 %collective-permute-start.1 = (f32[10,1,128]{2,1,0:T(1,128)}, f32[10,1,128]{2,1,0:T(1,128)S(1)}, u32[]{:S(2)}, u32[]{:S(2)}) collective-permute-start(f32[10,1,128]{2,1,0:T(1,128)} %bitcast.22), channel_id=1, source_target_pairs={{0,128},{128,0},{1,129},{129,1},{2,130},{130,2},{3,131},{131,3},{4... | collective-permute-start | bytes 15368 | tf_op jit(solution)/shard_map/ppermute | solution.py:226
  4.9 45.0 %copy-start.3 = (f32[1,10,128]{2,0,1:T(1,128)S(1)}, f32[1,10,128]{2,0,1:T(1,128)}, u32[]{:S(2)}) copy-start(f32[1,10,128]{2,0,1:T(1,128)} %param.17) | copy-start | bytes 15364
  4.9 70.1 %copy-start = (f32[1,1024,128]{2,1,0:T(8,128)S(1)}, f32[1,1024,128]{2,1,0:T(8,128)}, u32[]{:S(2)}) copy-start(f32[1,1024,128]{2,1,0:T(8,128)} %prod_second.1) | copy-start | bytes 1572868
  4.9 70.1 %copy-start.1 = (f32[1,10,1024]{2,0,1:T(1,128)S(1)}, f32[1,10,1024]{2,0,1:T(1,128)}, u32[]{:S(2)}) copy-start(f32[1,10,1024]{2,0,1:T(1,128)} %param.18) | copy-start | bytes 122884
  4.9 70.2 %copy-start.2 = (f32[128,32]{0,1:T(8,128)S(1)}, f32[128,32]{0,1:T(8,128)}, u32[]{:S(2)}) copy-start(f32[128,32]{0,1:T(8,128)} %param.21) | copy-start | bytes 49156
  4.9 70.1 %all-to-all-start = ((f32[128,1,2176]{2,1,0:T(1,128)}), f32[128,1,2176]{2,1,0:T(1,128)S(1)}, u32[]{:S(2)}, u32[]{:S(2)}) async-start(f32[128,1,2176]{2,1,0:T(1,128)} %bitcast.5), calls=%async_computation | async-start | bytes 2228224 | tf_op jit(solution)/shard_map/all_to_all | solution.py:262
  20.0 29.8 %collective-permute-start.2 = (f32[80,128]{1,0:T(8,128)S(1)}, f32[80,128]{1,0:T(8,128)S(1)}, u32[]{:S(2)}, u32[]{:S(2)}) collective-permute-start(f32[80,128]{1,0:T(8,128)S(1)} %get-tuple-element.23), channel_id=1, source_target_pairs={{0,16},{1,17},{2,18},{3,19},{4,20},{5,21},{6,22},{7,23},{8,24},{9,... | collective-permute-start | bytes 122888 | tf_op jit(solution)/shard_map/ppermute | solution.py:240
  49.9 1.2 %collective-permute-start.3 = (f32[80,128]{1,0:T(8,128)S(1)}, f32[80,128]{1,0:T(8,128)S(1)}, u32[]{:S(2)}, u32[]{:S(2)}) collective-permute-start(f32[80,128]{1,0:T(8,128)S(1)} %add.24), channel_id=1, source_target_pairs={{0,128},{128,0},{1,129},{129,1},{2,130},{130,2},{3,131},{131,3},{4... | collective-permute-start | bytes 122888 | tf_op jit(solution)/shard_map/ppermute | solution.py:226
  49.9 1.3 %collective-permute-start.4 = (f32[10,1,128]{2,1,0:T(1,128)S(1)}, f32[10,1,128]{2,1,0:T(1,128)S(1)}, u32[]{:S(2)}, u32[]{:S(2)}) collective-permute-start(f32[10,1,128]{2,1,0:T(1,128)S(1)} %bitcast.17), channel_id=1, source_target_pairs={{0,128},{128,0},{1,129},{129,1},{2,130},{130,2},{3,131},{131,3},{4... | collective-permute-start | bytes 15368 | tf_op jit(solution)/shard_map/ppermute | solution.py:226
  51.2 6.2 %collective-permute-start.5 = (f32[80,128]{1,0:T(8,128)S(1)}, f32[80,128]{1,0:T(8,128)S(1)}, u32[]{:S(2)}, u32[]{:S(2)}) collective-permute-start(f32[80,128]{1,0:T(8,128)S(1)} %add.25), channel_id=1, source_target_pairs={{0,2},{1,3},{2,0},{3,1},{4,6},{5,7},{6,4},{7,5},{8,10},{9,11},{10,... | collective-permute-start | bytes 122888 | tf_op jit(solution)/shard_map/ppermute | solution.py:240
  54.2 5.2 %collective-permute-start.6 = (f32[80,128]{1,0:T(8,128)S(1)}, f32[80,128]{1,0:T(8,128)S(1)}, u32[]{:S(2)}, u32[]{:S(2)}) collective-permute-start(f32[80,128]{1,0:T(8,128)S(1)} %add.25), channel_id=1, source_target_pairs={{0,1},{1,2},{2,3},{3,0},{4,5},{5,6},{6,7},{7,4},{8,9},{9,10},{10,1... | collective-permute-start | bytes 122888 | tf_op jit(solution)/shard_map/ppermute | solution.py:240
  54.8 4.6 %collective-permute-start.7 = (f32[80,128]{1,0:T(8,128)S(1)}, f32[80,128]{1,0:T(8,128)S(1)}, u32[]{:S(2)}, u32[]{:S(2)}) collective-permute-start(f32[80,128]{1,0:T(8,128)S(1)} %add.25), channel_id=1, source_target_pairs={{0,3},{1,0},{2,1},{3,2},{4,7},{5,4},{6,5},{7,6},{8,11},{9,8},{10,9... | collective-permute-start | bytes 122888 | tf_op jit(solution)/shard_map/ppermute | solution.py:240
  59.5 5.1 %collective-permute-start.10 = (f32[80,128]{1,0:T(8,128)S(1)}, f32[80,128]{1,0:T(8,128)S(1)}, u32[]{:S(2)}, u32[]{:S(2)}) collective-permute-start(f32[80,128]{1,0:T(8,128)S(1)} %add_add_fusion.1), channel_id=1, source_target_pairs={{0,96},{1,97},{2,98},{3,99},{4,100},{5,101},{6,102},{7,103},{8,104... | collective-permute-start | bytes 122888 | tf_op jit(solution)/shard_map/ppermute | solution.py:240
  62.9 5.5 %collective-permute-start.8 = (f32[80,128]{1,0:T(8,128)S(1)}, f32[80,128]{1,0:T(8,128)S(1)}, u32[]{:S(2)}, u32[]{:S(2)}) collective-permute-start(f32[80,128]{1,0:T(8,128)S(1)} %add_add_fusion.1), channel_id=1, source_target_pairs={{0,64},{1,65},{2,66},{3,67},{4,68},{5,69},{6,70},{7,71},{8,72},{9,... | collective-permute-start | bytes 122888 | tf_op jit(solution)/shard_map/ppermute | solution.py:240
  63.3 5.5 %collective-permute-start.9 = (f32[80,128]{1,0:T(8,128)S(1)}, f32[80,128]{1,0:T(8,128)S(1)}, u32[]{:S(2)}, u32[]{:S(2)}) collective-permute-start(f32[80,128]{1,0:T(8,128)S(1)} %add_add_fusion.1), channel_id=1, source_target_pairs={{0,32},{1,33},{2,34},{3,35},{4,36},{5,37},{6,38},{7,39},{8,40},{9,... | collective-permute-start | bytes 122888 | tf_op jit(solution)/shard_map/ppermute | solution.py:240
  68.8 6.2 %collective-permute-start.11 = (f32[80,128]{1,0:T(8,128)S(1)}, f32[80,128]{1,0:T(8,128)S(1)}, u32[]{:S(2)}, u32[]{:S(2)}) collective-permute-start(f32[80,128]{1,0:T(8,128)S(1)} %add_add_fusion.w_0), channel_id=1, source_target_pairs={{0,8},{1,9},{2,10},{3,11},{4,12},{5,13},{6,14},{7,15},{8,16},{9,17... | collective-permute-start | bytes 122888 | tf_op jit(solution)/shard_map/ppermute | solution.py:240
  68.9 6.1 %collective-permute-start.12 = (f32[80,128]{1,0:T(8,128)S(1)}, f32[80,128]{1,0:T(8,128)S(1)}, u32[]{:S(2)}, u32[]{:S(2)}) collective-permute-start(f32[80,128]{1,0:T(8,128)S(1)} %add_add_fusion.w_0), channel_id=1, source_target_pairs={{0,4},{1,5},{2,6},{3,7},{4,8},{5,9},{6,10},{7,11},{8,12},{9,13},{1... | collective-permute-start | bytes 122888 | tf_op jit(solution)/shard_map/ppermute | solution.py:240
  69.0 6.0 %collective-permute-start.13 = (f32[80,128]{1,0:T(8,128)S(1)}, f32[80,128]{1,0:T(8,128)S(1)}, u32[]{:S(2)}, u32[]{:S(2)}) collective-permute-start(f32[80,128]{1,0:T(8,128)S(1)} %add_add_fusion.w_0), channel_id=1, source_target_pairs={{0,28},{1,29},{2,30},{3,31},{4,0},{5,1},{6,2},{7,3},{8,4},{9,5},{1... | collective-permute-start | bytes 122888 | tf_op jit(solution)/shard_map/ppermute | solution.py:240
